TPU v7x, 32 devices: a whole 2x2x4 slice. The times are simulated.
32 devices in a mesh: grp: 2 (over x), seq: 8 (over z, y), head: 2 (over core).
Axes of the slice: x: 2, y: 2, z: 4, core: 2. Of those that a mesh axis runs over, the one named last changes fastest.
Arguments:
- query: bfloat16 [2048, 4096], P(('grp', 'seq'), 'head'), parts along dimension 0, may hold values from -6 to 6
- keys: bfloat16 [2048, 4096], P(('grp', 'seq'), 'head'), parts along dimension 0, may hold values from -6 to 6
- values: bfloat16 [2048, 4096], P(('grp', 'seq'), 'head'), parts along dimension 0, may hold values from -6 to 6
- resid: bfloat16 [2048, 3072], P(('grp', 'seq'), 'head'), parts along dimension 0, may hold values from -6 to 6
- attn_gain: float32 [4096], P('head'), may hold values from 0.2 to 1.8
- out_weight: bfloat16 [4096, 3072], P('head', 'seq'), may hold values from -0.09375 to 0.09375
- moe_gain: float32 [3072], replicated, may hold values from 0.2 to 1.8
- routes: int32 [2048, 2], P(('grp', 'seq')), parts along dimension 0, may hold values from 0 to 7, all different within a row; in each aligned block of 128 rows (0 to 127, 128 to 255, ...) at most 36 rows name the same one
- route_weights: float32 [2048, 2], P(('grp', 'seq')), parts along dimension 0, may hold values from 0.2 to 1
- w_gate: bfloat16 [3072, 36864], P(None, ('seq', 'head')), may hold values from -0.109375 to 0.109375
- w_up: bfloat16 [3072, 36864], P(None, ('seq', 'head')), may hold values from -0.109375 to 0.109375
- w_down: bfloat16 [36864, 3072], P(('seq', 'head')), may hold values from -0.09375 to 0.09375
Outputs:
- mixed: bfloat16 [2048, 3072], P(('grp', 'seq'), 'head'), parts along dimension 0
There are 2 independent parts, one for each index of `grp`. A program takes and returns all parts, laid end to end along the dimension named above; an argument that names none is the same for every part. Nothing has to cross between parts.
Inputs may be any that keep to these rules, and one draw needn't show every extreme that they name: A token's 2 experts differ. Within each aligned block of 128 tokens no expert is named by more than 36 routes, and in every draw some expert is named by exactly 36 routes of some block.
All inputs are finite; a program needn't handle non-finite values.
Results may differ from a plain program's by a relative error of at most 0.015.
Values may be sent and summed in bfloat16 or wider, within the bound.
A program may use at most 128 MiB of HBM per device.

v0:
```python
import functools

import jax
import jax.numpy as jnp
from jax import lax
from jax.experimental import pallas as pl
from jax.experimental.pallas import tpu as pltpu
from jax.sharding import PartitionSpec as P

D = 3072
HD = 128
EXPERTS = 8
TOP = 2
CAP = 36


EPS = 1e-06


def swap_heads(x):
    pairs = [(i, lax.axis_size("head") - 1 - i) for i in range(lax.axis_size("head"))]
    return lax.ppermute(x, "head", pairs)


def greet_all(me, count, pair=False):
    barrier = pltpu.get_barrier_semaphore()

    def greet(step, carry):
        pl.semaphore_signal(
            barrier,
            inc=1,
            device_id={"seq": lax.rem(me + step, count)},
            device_id_type=pl.DeviceIdType.MESH,
        )
        return carry

    lax.fori_loop(1, count, greet, 0)
    if pair:
        pl.semaphore_signal(
            barrier,
            inc=1,
            device_id={"head": 1 - lax.axis_index("head")},
            device_id_type=pl.DeviceIdType.MESH,
        )
    pl.semaphore_wait(barrier, count - 1 + int(pair))


def grant(*blocks):
    total = 1 << 20
    for shape in blocks:
        cells = (-(-shape[-1] // 128) * 128) * (-(-shape[-2] // 16) * 16)
        for size in shape[:-2]:
            cells = cells * size
        total = total + 2 * cells
    return total


def send_to(src, dst, send_sem, recv_sem, **device):
    return pltpu.make_async_remote_copy(
        src_ref=src,
        dst_ref=dst,
        send_sem=send_sem,
        recv_sem=recv_sem,
        device_id=device,
        device_id_type=pl.DeviceIdType.MESH,
    )


def sums_kernel(count, own_ref, out_ref, got, made, send_sem, recv_sem, home_send, home_recv):
    me = lax.axis_index("seq")
    greet_all(me, count)

    def out(other):
        return send_to(
            own_ref.at[other], got.at[me], send_sem.at[other], recv_sem.at[me], seq=other
        )

    def arrival(other):
        return send_to(
            own_ref.at[other], got.at[other], send_sem.at[other], recv_sem.at[other], seq=other
        )

    def home(other):
        return send_to(
            made.at[other], out_ref.at[me], home_send.at[other], home_recv.at[me], seq=other
        )

    def home_arrival(other):
        return send_to(
            made.at[other], out_ref.at[other], home_send.at[other], home_recv.at[other], seq=other
        )

    def start(step, carry):
        out(lax.rem(me + step, count)).start()
        return carry

    lax.fori_loop(1, count, start, 0)
    got[me] = own_ref[me]

    def add(block, running):
        made[block] = running.astype(jnp.bfloat16)

        @pl.when(block != me)
        def _():
            arrival(block).wait_recv()
            home(block).start()

        return running + got[block].astype(jnp.float32)

    lax.fori_loop(0, count, add, jnp.zeros(got.shape[1:], jnp.float32))
    out_ref[me] = made[me]

    def finish(step, carry):
        other = lax.rem(me + step, count)
        out(other).wait_send()
        home_arrival(other).wait_recv()
        home(other).wait_send()
        return carry

    lax.fori_loop(1, count, finish, 0)


def earlier_sums(own):
    count = lax.axis_size("seq")
    shape = (count, own.shape[0] // count, own.shape[1])
    return pl.pallas_call(
        functools.partial(sums_kernel, count),
        name="sums",
        out_shape=jax.ShapeDtypeStruct(shape, jnp.bfloat16),
        in_specs=[pl.BlockSpec(memory_space=pltpu.VMEM)],
        out_specs=pl.BlockSpec(memory_space=pltpu.VMEM),
        scratch_shapes=[pltpu.VMEM(shape, jnp.bfloat16)] * 2
        + [pltpu.SemaphoreType.DMA((count,))] * 4,
        compiler_params=pltpu.CompilerParams(
            collective_id=1, has_side_effects=True, vmem_limit_bytes=grant(shape, shape, shape, shape, shape)
        ),
    )(own.reshape(shape)).reshape(own.shape)


def dispatch_kernel(
    count, packed_ref, rows_ref, send_sem, recv_sem, pair_send, pair_recv, own_sem
):
    me, head = lax.axis_index("seq"), lax.axis_index("head")
    half = packed_ref.shape[2]
    greet_all(me, count, True)

    def place(source, side):
        return rows_ref.at[source, :, pl.ds(pl.multiple_of(side * half, 128), half)]

    def out(other):
        return send_to(
            packed_ref.at[other], place(me, head), send_sem.at[other], recv_sem.at[me], seq=other
        )

    def arrival(other):
        return send_to(
            packed_ref.at[other],
            place(other, head),
            send_sem.at[other],
            recv_sem.at[other],
            seq=other,
        )

    def pair(source, src, side):
        return send_to(
            src, place(source, side), pair_send.at[source], pair_recv.at[source], head=1 - head
        )

    def start(step, carry):
        out(lax.rem(me + step, count)).start()
        return carry

    lax.fori_loop(1, count, start, 0)
    own = pltpu.make_async_copy(packed_ref.at[me], place(me, head), own_sem)
    own.start()
    pair(me, packed_ref.at[me], head).start()

    def hand_on(step, carry):
        source = lax.rem(me - step + count, count)
        arrival(source).wait_recv()
        pair(source, place(source, head), head).start()
        return carry

    lax.fori_loop(1, count, hand_on, 0)
    own.wait()

    def finish(source, carry):
        pair(source, place(source, head), head).wait_send()
        pair(source, place(source, 1 - head), 1 - head).wait_recv()

        @pl.when(source != me)
        def _():
            out(source).wait_send()

        return carry

    lax.fori_loop(0, count, finish, 0)


def dispatch(packed):
    count, slots, half = packed.shape
    return pl.pallas_call(
        functools.partial(dispatch_kernel, count),
        name="dispatch",
        out_shape=jax.ShapeDtypeStruct((count, slots, 2 * half), jnp.bfloat16),
        in_specs=[pl.BlockSpec(memory_space=pltpu.VMEM)],
        out_specs=pl.BlockSpec(memory_space=pltpu.VMEM),
        scratch_shapes=[pltpu.SemaphoreType.DMA((count,))] * 4 + [pltpu.SemaphoreType.DMA],
        compiler_params=pltpu.CompilerParams(
            collective_id=2, has_side_effects=True, vmem_limit_bytes=grant((count, slots, 3 * half))
        ),
    )(packed)


def combine_kernel(
    count, part_ref, back_ref, theirs, total, send_sem, recv_sem, pair_send, pair_recv
):
    me, head = lax.axis_index("seq"), lax.axis_index("head")
    half = back_ref.shape[2]
    greet_all(me, count, True)

    def pair(block):
        columns = pl.ds(pl.multiple_of((1 - head) * half, 128), half)
        return send_to(
            part_ref.at[block, :, columns],
            theirs.at[block],
            pair_send.at[block],
            pair_recv.at[block],
            head=1 - head,
        )

    def home(other):
        return send_to(
            total.at[other], back_ref.at[me], send_sem.at[other], recv_sem.at[me], seq=other
        )

    def home_arrival(other):
        return send_to(
            total.at[other], back_ref.at[other], send_sem.at[other], recv_sem.at[other], seq=other
        )

    def start(step, carry):
        pair(lax.rem(me + step, count)).start()
        return carry

    lax.fori_loop(1, count + 1, start, 0)
    kept = pl.ds(pl.multiple_of(head * half, 128), half)

    def add(step, carry):
        block = lax.rem(me + step, count)
        pair(block).wait_recv()
        total[block] = (
            part_ref[block, :, kept].astype(jnp.float32) + theirs[block].astype(jnp.float32)
        ).astype(jnp.bfloat16)

        @pl.when(block != me)
        def _():
            home(block).start()

        return carry

    lax.fori_loop(1, count + 1, add, 0)
    back_ref[me] = total[me]

    def finish(block, carry):
        pair(block).wait_send()

        @pl.when(block != me)
        def _():
            home_arrival(block).wait_recv()
            home(block).wait_send()

        return carry

    lax.fori_loop(0, count, finish, 0)


def combine(part):
    count, slots, width = part.shape
    shape = (count, slots, width // 2)
    return pl.pallas_call(
        functools.partial(combine_kernel, count),
        name="combine",
        out_shape=jax.ShapeDtypeStruct(shape, jnp.bfloat16),
        in_specs=[pl.BlockSpec(memory_space=pltpu.VMEM)],
        out_specs=pl.BlockSpec(memory_space=pltpu.VMEM),
        scratch_shapes=[pltpu.VMEM(shape, jnp.bfloat16)] * 2
        + [pltpu.SemaphoreType.DMA((count,))] * 4,
        compiler_params=pltpu.CompilerParams(
            collective_id=3, has_side_effects=True, vmem_limit_bytes=grant(shape, shape, shape, part.shape, shape[1:])
        ),
    )(part)


def project_kernel(
    count, shard_ref, weight_ref, back_ref, held, made, send_sem, recv_sem, back_send, back_recv, own_sem
):
    me = lax.axis_index("seq")
    outer, inner = me // 2, lax.rem(me, 2)
    outers = count // 2
    partner = outer * 2 + (1 - inner)
    greet_all(me, count)

    def pass_on(source, src, way, to):
        return pltpu.make_async_remote_copy(
            src_ref=src,
            dst_ref=held.at[source],
            send_sem=send_sem.at[source, way],
            recv_sem=recv_sem.at[source],
            device_id={"seq": to},
            device_id_type=pl.DeviceIdType.MESH,
        )

    def go_home(source):
        return pltpu.make_async_remote_copy(
            src_ref=made.at[source],
            dst_ref=back_ref.at[me],
            send_sem=back_send.at[source],
            recv_sem=back_recv.at[me],
            device_id={"seq": source},
            device_id_type=pl.DeviceIdType.MESH,
        )

    def multiply(source, block):
        made[source] = jnp.dot(
            block[...], weight_ref[...], preferred_element_type=jnp.float32
        ).astype(jnp.bfloat16)

    @pl.when(outer + 1 < outers)
    def _():
        pass_on(me, shard_ref, 0, me + 2).start()

    @pl.when(outer > 0)
    def _():
        pass_on(me, shard_ref, 1, me - 2).start()

    pass_on(me, shard_ref, 2, partner).start()
    multiply(me, shard_ref)
    own = pltpu.make_async_copy(made.at[me], back_ref.at[me], own_sem)
    own.start()

    def arrive(source):
        pass_on(source, held.at[source], 2, partner).wait_recv()

    def take(source):
        multiply(source, held.at[source])
        go_home(source).start()

    def step(distance, carry):
        low, high = me - 2 * distance, me + 2 * distance

        @pl.when(outer - distance >= 0)
        def _():
            arrive(low)

            @pl.when(outer + 1 < outers)
            def _():
                pass_on(low, held.at[low], 0, me + 2).start()

            pass_on(low, held.at[low], 2, partner).start()
            take(low)

        @pl.when(outer + distance < outers)
        def _():
            arrive(high)

            @pl.when(outer > 0)
            def _():
                pass_on(high, held.at[high], 1, me - 2).start()

            pass_on(high, held.at[high], 2, partner).start()
            take(high)

        for source in (
            jnp.where(outer - (distance - 1) >= 0, partner - 2 * (distance - 1), -1),
            jnp.where(
                (distance > 1) & (outer + (distance - 1) < outers), partner + 2 * (distance - 1), -1
            ),
        ):

            @pl.when(source >= 0)
            def _():
                arrive(source)
                take(source)

        return carry

    lax.fori_loop(1, outers + 1, step, 0)
    own.wait()

    def finish(step, carry):
        source = lax.rem(me + step, count)
        go_home(source).wait_send()
        pltpu.make_async_remote_copy(
            src_ref=made.at[source],
            dst_ref=back_ref.at[source],
            send_sem=back_send.at[source],
            recv_sem=back_recv.at[source],
            device_id={"seq": source},
            device_id_type=pl.DeviceIdType.MESH,
        ).wait_recv()
        return carry

    lax.fori_loop(1, count, finish, 0)

    def drain(step, carry):
        source = step * 2 + inner

        @pl.when((source <= me) & (outer + 1 < outers))
        def _():
            pass_on(source, held.at[source], 0, me + 2).wait_send()

        @pl.when((source >= me) & (outer > 0))
        def _():
            pass_on(source, held.at[source], 1, me - 2).wait_send()

        pass_on(source, held.at[source], 2, partner).wait_send()
        return carry

    lax.fori_loop(0, outers, drain, 0)


def project(normed, out_weight):
    count = lax.axis_size("seq")
    rows, width = normed.shape
    columns = out_weight.shape[1]
    return pl.pallas_call(
        functools.partial(project_kernel, count),
        name="project",
        out_shape=jax.ShapeDtypeStruct((count, rows, columns), jnp.bfloat16),
        in_specs=[pl.BlockSpec(memory_space=pltpu.VMEM)] * 2,
        out_specs=pl.BlockSpec(memory_space=pltpu.VMEM),
        scratch_shapes=[
            pltpu.VMEM((count, rows, width), jnp.bfloat16),
            pltpu.VMEM((count, rows, columns), jnp.bfloat16),
            pltpu.SemaphoreType.DMA((count, 3)),
            pltpu.SemaphoreType.DMA((count,)),
            pltpu.SemaphoreType.DMA((count,)),
            pltpu.SemaphoreType.DMA((count,)),
            pltpu.SemaphoreType.DMA,
        ],
        compiler_params=pltpu.CompilerParams(
            collective_id=0,
            has_side_effects=True,
            vmem_limit_bytes=grant(
                (count + 1, rows, width), (2 * count + 8, rows, columns), out_weight.shape
            ),
        ),
    )(normed, out_weight)


def per_device(
    query,
    keys,
    values,
    resid,
    attn_gain,
    out_weight,
    moe_gain,
    routes,
    route_weights,
    w_gate,
    w_up,
    w_down,
):
    tok_rows = query.shape[0]
    local_heads = query.shape[1] // HD
    seq_count = lax.axis_size("seq")
    head_count = lax.axis_size("head")
    head_pos = lax.axis_index("head")
    half_width = D // head_count
    slices = seq_count * head_count // EXPERTS
    q_three = query.reshape(tok_rows, local_heads, HD)
    k_three = keys.reshape(tok_rows, local_heads, HD)
    value_three_dims = values.reshape(tok_rows, local_heads, HD)
    block_own_state = jnp.einsum(
        "tnd,tne->nde", k_three, value_three_dims, preferred_element_type=jnp.float32
    )
    earlier = earlier_sums(
        block_own_state.astype(jnp.bfloat16).reshape(local_heads * HD, HD)
    ).reshape(local_heads, HD, HD)
    inter = jnp.einsum("tnd,nde->tne", q_three, earlier, preferred_element_type=jnp.float32)
    scores = jnp.einsum("tnd,snd->nts", q_three, k_three, preferred_element_type=jnp.float32)
    causal = jnp.arange(tok_rows)[:, None] >= jnp.arange(tok_rows)[None, :]
    resident_weight_parts = jnp.where(causal, scores, 0.0).astype(jnp.bfloat16)
    inside_block_scores = jnp.einsum(
        "rbj,jrh->brh", resident_weight_parts, value_three_dims, preferred_element_type=jnp.float32
    )
    attention = inter + inside_block_scores
    scale = lax.rsqrt(jnp.mean(attention * attention, axis=-1, keepdims=True) + EPS)
    normed = (
        (attention * scale * attn_gain.reshape(local_heads, HD))
        .astype(jnp.bfloat16)
        .reshape(tok_rows, local_heads * HD)
    )
    projected = (
        project(normed, out_weight).transpose(1, 0, 2).reshape(tok_rows, D).astype(jnp.float32)
    )
    placed = lax.dynamic_update_slice_in_dim(
        jnp.zeros((tok_rows, D), jnp.float32), resid.astype(jnp.float32), head_pos * half_width, 1
    )
    half = (projected + placed).astype(jnp.bfloat16)
    other = swap_heads(half)
    hidden = (half.astype(jnp.float32) + other.astype(jnp.float32)).astype(jnp.bfloat16)
    wide = hidden.astype(jnp.float32)
    moe_in = (
        wide * lax.rsqrt(jnp.mean(wide * wide, axis=-1, keepdims=True) + EPS) * moe_gain
    ).astype(jnp.bfloat16)
    own_rows = lax.dynamic_slice_in_dim(wide, head_pos * half_width, half_width, 1)
    flat_routes = routes.reshape(-1)
    onehot = (flat_routes[:, None] == jnp.arange(EXPERTS, dtype=jnp.int32)[None, :]).astype(
        jnp.int32
    )
    slots = jnp.sum((jnp.cumsum(onehot, axis=0) - 1) * onehot, axis=1)
    targets = (flat_routes * CAP + slots).reshape(tok_rows, TOP)
    slot_columns = jnp.arange(EXPERTS * CAP, dtype=jnp.int32)
    chosen = (targets[:, :, None] == slot_columns[None, None, :]).astype(jnp.float32)
    picker = jnp.sum(chosen, axis=1).astype(jnp.bfloat16)
    combine_weights = jnp.sum(chosen * route_weights[:, :, None], axis=1)
    contract_rows = (((0,), (0,)), ((), ()))
    own_half = lax.dynamic_slice_in_dim(moe_in, head_pos * half_width, half_width, 1)
    packed = lax.dot_general(
        picker, own_half, contract_rows, preferred_element_type=jnp.float32
    ).astype(jnp.bfloat16)
    chips = slices // head_count
    copies = jnp.broadcast_to(
        packed.reshape(EXPERTS, 1, CAP, half_width), (EXPERTS, chips, CAP, half_width)
    ).reshape(EXPERTS * chips, CAP, half_width)
    rows_in = dispatch(copies).reshape(-1, D)
    gate = jnp.dot(rows_in, w_gate, preferred_element_type=jnp.float32)
    upward = jnp.dot(rows_in, w_up, preferred_element_type=jnp.float32)
    inner = (jax.nn.silu(gate) * upward).astype(jnp.bfloat16)
    inner = lax.optimization_barrier(inner)
    part = jnp.dot(inner, w_down, preferred_element_type=jnp.float32).astype(jnp.bfloat16)
    back = combine(part.reshape(seq_count, CAP, D)).reshape(EXPERTS, chips, CAP, half_width)
    high = combine_weights.astype(jnp.bfloat16)
    low = (combine_weights - high.astype(jnp.float32)).astype(jnp.bfloat16)
    moe_out = jnp.zeros((tok_rows, half_width), jnp.float32)
    for chip in range(chips):
        piece = back[:, chip].reshape(EXPERTS * CAP, half_width)
        moe_out = moe_out + jnp.dot(high, piece, preferred_element_type=jnp.float32)
        moe_out = moe_out + jnp.dot(low, piece, preferred_element_type=jnp.float32)
    return (own_rows + moe_out).astype(jnp.bfloat16)


def solution(mesh):
    return jax.shard_map(
        per_device,
        mesh=mesh,
        in_specs=(
            P(("grp", "seq"), "head"),
            P(("grp", "seq"), "head"),
            P(("grp", "seq"), "head"),
            P(("grp", "seq"), "head"),
            P("head"),
            P("head", "seq"),
            P(),
            P(("grp", "seq"), None),
            P(("grp", "seq"), None),
            P(None, ("seq", "head")),
            P(None, ("seq", "head")),
            P(("seq", "head"), None),
        ),
        out_specs=P(("grp", "seq"), "head"),
        check_vma=False,
    )
```

profile of v0, /device:TPU:27, one launch (start us, length us, event | category | flops | bytes accessed | tf_op | source)
XLA Modules:
  0.0 184.5 jit_solution(8764536744116869208)
XLA Ops:
  0.0 0.0 copy-start.5
  0.0 1.4 copy.67
  1.4 0.5 convolution_convert_fusion.2
  2.0 25.1 %sums.1 = bf16[8,256,128]{2,1,0:T(8,128)(2,1)S(1)} custom-call(bf16[8,256,128]{2,1,0:T(8,128)(2,1)S(1)} %bitcast.64), custom_call_target="tpu_custom_call" | custom-call | tf_op jit(solution)/shard_map/sums/pallas_call | solution.py:126
  27.1 0.5 convolution_bitcast_fusion.1
  27.6 1.9 %multiply_reduce_fusion.1 = (f32[128,16]{0,1:T(8,128)S(1)}, f32[128,16,128]{0,2,1:T(8,128)S(1)}) fusion(f32[128,16,128]{0,2,1:T(8,128)S(1)} %convolution_bitcast_fusion.1, bf16[128,16,128]{0,2,1:T(8,128)(2,1)S(1)} %bitcast.68, pred[128,128]{1,0:T(8,128)(4,1)S(1)} %iota_compare_fusion.1, bf16[128,2048]{1,0:T(8,128)(2,1)} %param.12, ...), kind=kOutput, calls=%fused_computation.17 | convolution fusion | flops 135526400 | bytes 3694592 | tf_op jit(solution)/shard_map/rbj,jrh->brh/dot_general | solution.py:486
  29.5 0.0 copy-start.2
  29.6 1.1 multiply_convert_fusion
  30.7 1.2 copy.66.shard_ref
  31.9 59.5 %project.1 = bf16[8,128,384]{2,1,0:T(8,128)(2,1)S(1)} custom-call(bf16[128,2048]{1,0:T(8,128)(2,1)S(1)} %copy.66.shard_ref, bf16[2048,384]{1,0:T(8,128)(2,1)S(1)} %copy-done.2), custom_call_target="tpu_custom_call" | custom-call | tf_op jit(solution)/shard_map/project/pallas_call | solution.py:427
  91.5 0.1 convert_bitcast_fusion
  91.6 0.5 copy.59
  92.1 0.0 copy-start.7
  92.1 0.5 copy.61
  92.5 0.5 copy-done.7
  93.1 0.1 add_dynamic-update-slice_fusion
  93.2 0.0 copy-start.9
  93.2 0.0 copy-start.11
  93.2 1.0 convert_element_type.81
  94.2 4.8 %collective-permute-start = (bf16[128,3072]{1,0:T(8,128)(2,1)}, bf16[128,3072]{1,0:T(8,128)(2,1)S(1)}, u32[]{:S(2)}, u32[]{:S(2)}) collective-permute-start(bf16[128,3072]{1,0:T(8,128)(2,1)} %convert_element_type.81), channel_id=1, source_target_pairs={{0,1},{1,0},{2,3},{3,2},{4,5},{5,4},{6,7},{7,6},{8,9},{9,8},{10,11... | collective-permute-start | bytes 2359304 | tf_op jit(solution)/shard_map/ppermute | solution.py:22
  99.0 0.1 copy.62
  99.1 0.1 eq.42
  99.2 0.1 eq.38
  99.4 0.1 dynamic-slice.1
  99.5 0.6 reduce-window.6
  100.1 0.2 slice_reduce_fusion
  100.3 0.1 fusion.26
  100.4 0.1 reduce_sum.49
  100.6 0.1 copy.64
  100.6 0.1 select_reduce_fusion
  100.7 0.4 collective-permute-done
  101.1 0.3 multiply_reduce_fusion
  101.5 1.1 copy-done.3
  102.6 0.5 convolution_convert_fusion.1
  103.1 0.2 reshape_reshape.11.packed_ref
  103.2 26.2 %dispatch.1 = bf16[8,36,3072]{2,1,0:T(8,128)(2,1)S(1)} custom-call(bf16[8,36,1536]{2,1,0:T(8,128)(2,1)S(1)} %reshape_reshape.11.packed_ref), custom_call_target="tpu_custom_call" | custom-call | tf_op jit(solution)/shard_map/dispatch/pallas_call | solution.py:202
  129.4 1.4 reshape.71
  130.8 8.7 %fusion.34 = f32[288,2304]{1,0:T(8,128)S(1)} fusion(bf16[288,3072]{1,0:T(8,128)(2,1)} %reshape.71, bf16[3072,2304]{1,0:T(8,128)(2,1)} %param.21), kind=kOutput, calls=%fused_computation.53 | convolution fusion | flops 4076863488 | bytes 18579456 | tf_op jit(solution)/shard_map/dot_general | solution.py:530
  139.6 0.0 slice-start.2
  139.6 9.6 %fusion = bf16[288,2304]{1,0:T(8,128)(2,1)S(1)} fusion(bf16[288,3072]{1,0:T(8,128)(2,1)S(1)} %copy-done.6, bf16[3072,2304]{1,0:T(8,128)(2,1)} %param.22, f32[288,2304]{1,0:T(8,128)S(1)} %fusion.34), kind=kOutput, calls=%fused_computation.1 | convolution fusion | flops 4080844800 | bytes 19906560 | tf_op jit(solution)/shard_map/dot_general | solution.py:531
  149.3 5.5 %convolution_convert_fusion = bf16[288,3072]{1,0:T(8,128)(2,1)} fusion(bf16[288,2304]{1,0:T(8,128)(2,1)S(1)} %fusion, bf16[2304,3072]{1,0:T(8,128)(2,1)S(1)} %bitcast.72), kind=kOutput, calls=%fused_computation.2 | convolution fusion | flops 4077748224 | bytes 17252352 | tf_op jit(solution)/shard_map/dot_general | solution.py:534
  154.8 1.6 reshape.72.part_ref
  156.4 25.3 %combine.1 = bf16[8,36,1536]{2,1,0:T(8,128)(2,1)S(1)} custom-call(bf16[8,36,3072]{2,1,0:T(8,128)(2,1)S(1)} %reshape.72.part_ref), custom_call_target="tpu_custom_call" | custom-call | tf_op jit(solution)/shard_map/combine/pallas_call | solution.py:281
  181.7 0.2 reshape_squeeze_reshape.3
  181.9 0.0 copy-start.1
  181.9 0.4 fusion.24
  182.3 1.0 copy-done.4
  183.3 1.1 fusion.2
  (30 shorter events, 0.1 us)
Async XLA Ops:
  0.0 1.4 copy-start
  0.0 27.1 %copy-start.5 = (bf16[128,2048]{1,0:T(8,128)(2,1)S(1)}, bf16[128,2048]{1,0:T(8,128)(2,1)}, u32[]{:S(2)}) copy-start(bf16[128,2048]{1,0:T(8,128)(2,1)} %param.12) | copy-start | bytes 1572868
  27.6 1.9 %copy-start.8 = (f32[2048]{0:T(1024)S(1)}, f32[2048]{0:T(1024)}, u32[]{:S(2)}) copy-start(f32[2048]{0:T(1024)} %param.16) | copy-start | bytes 24580
  29.5 2.4 %copy-start.2 = (bf16[2048,384]{1,0:T(8,128)(2,1)S(1)}, bf16[2048,384]{1,0:T(8,128)(2,1)}, u32[]{:S(2)}) copy-start(bf16[2048,384]{1,0:T(8,128)(2,1)} %weight_ref.1) | copy-start | bytes 4718596
  92.1 1.0 copy-start.7
  93.1 5.9 %copy-start.10 = (s32[128,2]{0,1:T(2,128)S(1)}, s32[128,2]{0,1:T(2,128)}, u32[]{:S(2)}) copy-start(s32[128,2]{0,1:T(2,128)} %param.19) | copy-start | bytes 3076
  93.2 6.2 %copy-start.9 = (f32[3072]{0:T(1024)S(1)}, f32[3072]{0:T(1024)}, u32[]{:S(2)}) copy-start(f32[3072]{0:T(1024)} %param.18) | copy-start | bytes 36868
  93.2 7.4 %copy-start.11 = (f32[128,2]{0,1:T(2,128)S(1)}, f32[128,2]{0,1:T(2,128)}, u32[]{:S(2)}) copy-start(f32[128,2]{0,1:T(2,128)} %param.20) | copy-start | bytes 3076
  94.2 6.9 %collective-permute-start = (bf16[128,3072]{1,0:T(8,128)(2,1)}, bf16[128,3072]{1,0:T(8,128)(2,1)S(1)}, u32[]{:S(2)}, u32[]{:S(2)}) collective-permute-start(bf16[128,3072]{1,0:T(8,128)(2,1)} %convert_element_type.81), channel_id=1, source_target_pairs={{0,1},{1,0},{2,3},{3,2},{4,5},{5,4},{6,7},{7,6},{8,9},{9,8},{10,11... | collective-permute-start | bytes 2359304 | tf_op jit(solution)/shard_map/ppermute | solution.py:22
  101.4 1.2 copy-start.3
  130.8 8.8 %copy-start.6 = (bf16[288,3072]{1,0:T(8,128)(2,1)S(1)}, bf16[288,3072]{1,0:T(8,128)(2,1)}, u32[]{:S(2)}) copy-start(bf16[288,3072]{1,0:T(8,128)(2,1)} %reshape.71) | copy-start | bytes 5308420
  130.8 18.4 %slice-start = ((s8[14155776]{0:T(1024)(128)(4,1)}), s8[4194304]{0:T(1024)(128)(4,1)S(1)}, s32[]{:S(2)}) async-start(s8[14155776]{0:T(1024)(128)(4,1)} %bitcast.71), calls=%async_computation | async-start | bytes 8388608
  130.8 18.4 %slice-start.1 = ((s8[14155776]{0:T(1024)(128)(4,1)}), s8[4194304]{0:T(1024)(128)(4,1)S(1)}, s32[]{:S(2)}) async-start(s8[14155776]{0:T(1024)(128)(4,1)} %bitcast.71), calls=%async_computation.1 | async-start | bytes 8388608
  139.6 9.6 %slice-start.2 = ((s8[14155776]{0:T(1024)(128)(4,1)}), s8[4194304]{0:T(1024)(128)(4,1)S(1)}, s32[]{:S(2)}) async-start(s8[14155776]{0:T(1024)(128)(4,1)} %bitcast.71), calls=%async_computation.2 | async-start | bytes 8388608
  139.6 9.6 %slice-start.3 = ((s8[14155776]{0:T(1024)(128)(4,1)}), s8[1572864]{0:T(1024)(128)(4,1)S(1)}, s32[]{:S(2)}) async-start(s8[14155776]{0:T(1024)(128)(4,1)} %bitcast.71), calls=%async_computation.3 | async-start | bytes 3145728
  181.9 1.4 copy-start.4
  181.9 2.5 %copy-start.1 = (bf16[128,2048]{1,0:T(8,128)(2,1)S(1)}, bf16[128,2048]{1,0:T(8,128)(2,1)}, u32[]{:S(2)}) copy-start(bf16[128,2048]{1,0:T(8,128)(2,1)} %param.13) | copy-start | bytes 1572868
where the time goes:
time: 188 us; the launch traced here: 184 us
  Pallas kernels  136 us (72%)
  matrix products  28.8 us (15%)
  local copies, waits for them, and re-layouts  10.6 us (6%)
  starting transfers between devices  4.8 us (3%)
  other arithmetic  3.48 us (2%)
    pallas_call x1, Pallas kernels, project(): pl.pallas_call(functools.partial(project_kernel, count), name='project',...  59.5 us
    pallas_call x1, Pallas kernels, dispatch(): pl.pallas_call(functools.partial(dispatch_kernel, count), name='dispatch'...  26.2 us
    pallas_call x1, Pallas kernels, combine(): pl.pallas_call(functools.partial(combine_kernel, count), name='combine',...  25.3 us
    pallas_call x1, Pallas kernels, earlier_sums(): pl.pallas_call(functools.partial(sums_kernel, count), name='sums', out_sh...  25.1 us
    dot_general x1, matrix products, per_device(): upward = jnp.dot(rows_in, w_up, preferred_element_type=jnp.float32)  9.59 us
    dot_general x1, matrix products, per_device(): gate = jnp.dot(rows_in, w_gate, preferred_element_type=jnp.float32)  8.75 us
    dot_general x1, matrix products, per_device(): jnp.dot(inner, w_down, preferred_element_type=jnp.float32)  5.55 us
    ppermute x1, starting transfers between devices, swap_heads(): return lax.ppermute(x, 'head', pairs)  4.8 us
  transfers between devices with their start and end apart: 1, of which 1 were waited for; matrix products, arithmetic and copies ran while one was open for 1% of the time, Pallas kernels for 0%

commit v1 on v0

--- a/solution.py
+++ b/solution.py
@@ -15,6 +15,7 @@
 
 
 EPS = 1e-06
+VMEM_MOST = 67043328
 
 
 def swap_heads(x):
@@ -137,159 +138,318 @@
     )(own.reshape(shape)).reshape(own.shape)
 
 
-def dispatch_kernel(
-    count, packed_ref, rows_ref, send_sem, recv_sem, pair_send, pair_recv, own_sem
+def tile_of(size, most):
+    fits = [n for n in range(128, min(size, most) + 1, 128) if size % n == 0]
+    return max(fits) if fits else size
+
+
+def experts_kernel(
+    count,
+    packed_ref,
+    own_ref,
+    high_ref,
+    low_ref,
+    gate_hbm,
+    up_hbm,
+    down_hbm,
+    mixed_ref,
+    rows,
+    x,
+    gate,
+    up,
+    inner,
+    w_gate,
+    w_up,
+    w_down,
+    mine,
+    theirs,
+    part,
+    total,
+    back,
+    send_sem,
+    recv_sem,
+    pair_send,
+    pair_recv,
+    part_send,
+    part_recv,
+    home_send,
+    home_recv,
+    gate_sem,
+    up_sem,
+    down_sem,
+    own_sem,
 ):
     me, head = lax.axis_index("seq"), lax.axis_index("head")
-    half = packed_ref.shape[2]
+    cap, half = packed_ref.shape[1], packed_ref.shape[2]
+    chunks, wide = rows.shape[1], rows.shape[4]
+    hidden = inner.shape[1]
+    tile = tile_of(hidden, 768)
+    group = 4
+    span = group * cap
+
+    def start_row(side, chunk):
+        return pl.multiple_of(jnp.where(side == 0, head, 1 - head) * half + chunk * wide, wide)
+
+    def weights(side, chunk):
+        ks = pl.ds(start_row(side, chunk), wide)
+        spot = chunk * 2 + side
+        return (
+            pltpu.make_async_copy(gate_hbm.at[ks], w_gate.at[ks], gate_sem.at[spot]),
+            pltpu.make_async_copy(up_hbm.at[ks], w_up.at[ks], up_sem.at[spot]),
+        )
+
+    down = pltpu.make_async_copy(down_hbm, w_down, down_sem)
+
+    def fetch(spot, carry):
+        for copy in weights(lax.rem(spot, 2), spot // 2):
+            copy.start()
+        return carry
+
+    lax.fori_loop(0, 2 * chunks, fetch, 0)
+    down.start()
     greet_all(me, count, True)
 
-    def place(source, side):
-        return rows_ref.at[source, :, pl.ds(pl.multiple_of(side * half, 128), half)]
-
-    def out(other):
-        return send_to(
-            packed_ref.at[other], place(me, head), send_sem.at[other], recv_sem.at[me], seq=other
-        )
-
-    def arrival(other):
-        return send_to(
-            packed_ref.at[other],
-            place(other, head),
-            send_sem.at[other],
-            recv_sem.at[other],
+    def chunk_of(chunk):
+        return pl.ds(pl.multiple_of(chunk * wide, wide), wide)
+
+    def out(chunk, other):
+        return send_to(
+            packed_ref.at[other, :, chunk_of(chunk)],
+            rows.at[0, chunk, me],
+            send_sem.at[chunk, other],
+            recv_sem.at[chunk, me],
             seq=other,
         )
 
-    def pair(source, src, side):
-        return send_to(
-            src, place(source, side), pair_send.at[source], pair_recv.at[source], head=1 - head
-        )
-
-    def start(step, carry):
-        out(lax.rem(me + step, count)).start()
-        return carry
-
-    lax.fori_loop(1, count, start, 0)
-    own = pltpu.make_async_copy(packed_ref.at[me], place(me, head), own_sem)
-    own.start()
-    pair(me, packed_ref.at[me], head).start()
-
-    def hand_on(step, carry):
-        source = lax.rem(me - step + count, count)
-        arrival(source).wait_recv()
-        pair(source, place(source, head), head).start()
-        return carry
-
-    lax.fori_loop(1, count, hand_on, 0)
-    own.wait()
-
-    def finish(source, carry):
-        pair(source, place(source, head), head).wait_send()
-        pair(source, place(source, 1 - head), 1 - head).wait_recv()
-
-        @pl.when(source != me)
-        def _():
-            out(source).wait_send()
-
-        return carry
-
-    lax.fori_loop(0, count, finish, 0)
-
-
-def dispatch(packed):
-    count, slots, half = packed.shape
+    def arrival(chunk, other):
+        return send_to(
+            packed_ref.at[other, :, chunk_of(chunk)],
+            rows.at[0, chunk, other],
+            send_sem.at[chunk, other],
+            recv_sem.at[chunk, other],
+            seq=other,
+        )
+
+    def keep(chunk):
+        return pltpu.make_async_copy(
+            packed_ref.at[me, :, chunk_of(chunk)], rows.at[0, chunk, me], own_sem.at[chunk]
+        )
+
+    def pair(chunk):
+        return send_to(
+            rows.at[0, chunk], rows.at[1, chunk], pair_send.at[chunk], pair_recv.at[chunk], head=1 - head
+        )
+
+    def post(chunk, carry):
+        def one(step, inside):
+            out(chunk, lax.rem(me + step, count)).start()
+            return inside
+
+        lax.fori_loop(1, count, one, 0)
+        keep(chunk).start()
+        return carry
+
+    lax.fori_loop(0, chunks, post, 0)
+    gate[...] = jnp.zeros_like(gate)
+    up[...] = jnp.zeros_like(up)
+
+    def join(pages):
+        return jnp.concatenate([page.astype(jnp.float32) for page in pages], axis=0).astype(jnp.bfloat16)
+
+    def gather(side, chunk):
+        def one(g, carry):
+            x[pl.ds(pl.multiple_of(g * span, 16), span), :] = join(
+                [rows[side, chunk, g * group + i] for i in range(group)]
+            )
+            return carry
+
+        lax.fori_loop(0, count // group, one, 0)
+
+    def accumulate(side, chunk):
+        for copy in weights(side, chunk):
+            copy.wait()
+        gather(side, chunk)
+        ks = pl.ds(start_row(side, chunk), wide)
+
+        def one(n, carry):
+            cols = pl.ds(pl.multiple_of(n * tile, tile), tile)
+            gate[:, cols] += jnp.dot(x[...], w_gate[ks, cols], preferred_element_type=jnp.float32)
+            up[:, cols] += jnp.dot(x[...], w_up[ks, cols], preferred_element_type=jnp.float32)
+            return carry
+
+        lax.fori_loop(0, hidden // tile, one, 0)
+
+    def take(chunk, carry):
+        def one(step, inside):
+            arrival(chunk, lax.rem(me + count - step, count)).wait_recv()
+            return inside
+
+        lax.fori_loop(1, count, one, 0)
+        keep(chunk).wait()
+        pair(chunk).start()
+        accumulate(0, chunk)
+        pair(chunk).wait_recv()
+        accumulate(1, chunk)
+        return carry
+
+    lax.fori_loop(0, chunks, take, 0)
+
+    small = tile_of(hidden, 256)
+
+    def activate(n, carry):
+        cols = pl.ds(pl.multiple_of(n * small, small), small)
+        inner[:, cols] = (jax.nn.silu(gate[:, cols]) * up[:, cols]).astype(jnp.bfloat16)
+        return carry
+
+    lax.fori_loop(0, hidden // small, activate, 0)
+    down.wait()
+
+    def hand(chunk):
+        return send_to(mine.at[chunk], theirs.at[chunk], part_send.at[chunk], part_recv.at[chunk], head=1 - head)
+
+    def home(chunk, other):
+        return send_to(
+            total.at[chunk, other],
+            back.at[chunk, me],
+            home_send.at[chunk, other],
+            home_recv.at[chunk, me],
+            seq=other,
+        )
+
+    def home_arrival(chunk, other):
+        return send_to(
+            total.at[chunk, other],
+            back.at[chunk, other],
+            home_send.at[chunk, other],
+            home_recv.at[chunk, other],
+            seq=other,
+        )
+
+    def project(side, chunk):
+        cols = pl.ds(start_row(side, chunk), wide)
+        part[...] = jnp.dot(inner[...], w_down[:, cols], preferred_element_type=jnp.float32)
+
+    def give(chunk, carry):
+        project(1, chunk)
+
+        def split(g, inside):
+            block = part[pl.ds(pl.multiple_of(g * span, 8), span), :]
+            for i in range(group):
+                mine[chunk, g * group + i] = block[i * cap : (i + 1) * cap].astype(jnp.bfloat16)
+            return inside
+
+        lax.fori_loop(0, count // group, split, 0)
+        hand(chunk).start()
+        project(0, chunk)
+        hand(chunk).wait_recv()
+
+        def add(g, inside):
+            block = part[pl.ds(pl.multiple_of(g * span, 8), span), :]
+            for i in range(group):
+                spot = g * group + i
+                total[chunk, spot] = (
+                    block[i * cap : (i + 1) * cap] + theirs[chunk, spot].astype(jnp.float32)
+                ).astype(jnp.bfloat16)
+            return inside
+
+        lax.fori_loop(0, count // group, add, 0)
+
+        def one(step, inside):
+            home(chunk, lax.rem(me + step, count)).start()
+            return inside
+
+        lax.fori_loop(1, count, one, 0)
+        back[chunk, me] = total[chunk, me]
+        return carry
+
+    lax.fori_loop(0, chunks, give, 0)
+
+    def mix(chunk, carry):
+        def one(step, inside):
+            home_arrival(chunk, lax.rem(me + count - step, count)).wait_recv()
+            return inside
+
+        lax.fori_loop(1, count, one, 0)
+
+        def pack(g, inside):
+            x[pl.ds(pl.multiple_of(g * span, 16), span), :] = join(
+                [back[chunk, g * group + i] for i in range(group)]
+            )
+            return inside
+
+        lax.fori_loop(0, count // group, pack, 0)
+        cols = chunk_of(chunk)
+        mixed_ref[:, cols] = (
+            own_ref[:, cols].astype(jnp.float32)
+            + jnp.dot(high_ref[...], x[...], preferred_element_type=jnp.float32)
+            + jnp.dot(low_ref[...], x[...], preferred_element_type=jnp.float32)
+        ).astype(jnp.bfloat16)
+        return carry
+
+    lax.fori_loop(0, chunks, mix, 0)
+
+    def finish(chunk, carry):
+        def one(step, inside):
+            other = lax.rem(me + step, count)
+            out(chunk, other).wait_send()
+            home(chunk, other).wait_send()
+            return inside
+
+        lax.fori_loop(1, count, one, 0)
+        pair(chunk).wait_send()
+        hand(chunk).wait_send()
+        return carry
+
+    lax.fori_loop(0, chunks, finish, 0)
+
+
+def experts(packed, own, high, low, w_gate, w_up, w_down):
+    count, cap, half = packed.shape
+    hidden = w_gate.shape[1]
+    wide = tile_of(half, 512)
+    chunks = half // wide
+    rows = count * cap
+    pages = (chunks, count, cap, wide)
+    dma = pltpu.SemaphoreType.DMA
+    vmem = pl.BlockSpec(memory_space=pltpu.VMEM)
+    hbm = pl.BlockSpec(memory_space=pl.ANY)
     return pl.pallas_call(
-        functools.partial(dispatch_kernel, count),
-        name="dispatch",
-        out_shape=jax.ShapeDtypeStruct((count, slots, 2 * half), jnp.bfloat16),
-        in_specs=[pl.BlockSpec(memory_space=pltpu.VMEM)],
-        out_specs=pl.BlockSpec(memory_space=pltpu.VMEM),
-        scratch_shapes=[pltpu.SemaphoreType.DMA((count,))] * 4 + [pltpu.SemaphoreType.DMA],
+        functools.partial(experts_kernel, count),
+        name="experts",
+        out_shape=jax.ShapeDtypeStruct(own.shape, jnp.bfloat16),
+        in_specs=[vmem] * 4 + [hbm] * 3,
+        out_specs=vmem,
+        scratch_shapes=[
+            pltpu.VMEM((2,) + pages, jnp.bfloat16),
+            pltpu.VMEM((rows, wide), jnp.bfloat16),
+            pltpu.VMEM((rows, hidden), jnp.float32),
+            pltpu.VMEM((rows, hidden), jnp.float32),
+            pltpu.VMEM((rows, hidden), jnp.bfloat16),
+            pltpu.VMEM(w_gate.shape, jnp.bfloat16),
+            pltpu.VMEM(w_up.shape, jnp.bfloat16),
+            pltpu.VMEM(w_down.shape, jnp.bfloat16),
+            pltpu.VMEM(pages, jnp.bfloat16),
+            pltpu.VMEM(pages, jnp.bfloat16),
+            pltpu.VMEM((rows, wide), jnp.float32),
+            pltpu.VMEM(pages, jnp.bfloat16),
+            pltpu.VMEM(pages, jnp.bfloat16),
+            dma((chunks, count)),
+            dma((chunks, count)),
+            dma((chunks,)),
+            dma((chunks,)),
+            dma((chunks,)),
+            dma((chunks,)),
+            dma((chunks, count)),
+            dma((chunks, count)),
+            dma((2 * chunks,)),
+            dma((2 * chunks,)),
+            dma,
+            dma((chunks,)),
+        ],
         compiler_params=pltpu.CompilerParams(
-            collective_id=2, has_side_effects=True, vmem_limit_bytes=grant((count, slots, 3 * half))
+            collective_id=2, has_side_effects=True, vmem_limit_bytes=VMEM_MOST
         ),
-    )(packed)
-
-
-def combine_kernel(
-    count, part_ref, back_ref, theirs, total, send_sem, recv_sem, pair_send, pair_recv
-):
-    me, head = lax.axis_index("seq"), lax.axis_index("head")
-    half = back_ref.shape[2]
-    greet_all(me, count, True)
-
-    def pair(block):
-        columns = pl.ds(pl.multiple_of((1 - head) * half, 128), half)
-        return send_to(
-            part_ref.at[block, :, columns],
-            theirs.at[block],
-            pair_send.at[block],
-            pair_recv.at[block],
-            head=1 - head,
-        )
-
-    def home(other):
-        return send_to(
-            total.at[other], back_ref.at[me], send_sem.at[other], recv_sem.at[me], seq=other
-        )
-
-    def home_arrival(other):
-        return send_to(
-            total.at[other], back_ref.at[other], send_sem.at[other], recv_sem.at[other], seq=other
-        )
-
-    def start(step, carry):
-        pair(lax.rem(me + step, count)).start()
-        return carry
-
-    lax.fori_loop(1, count + 1, start, 0)
-    kept = pl.ds(pl.multiple_of(head * half, 128), half)
-
-    def add(step, carry):
-        block = lax.rem(me + step, count)
-        pair(block).wait_recv()
-        total[block] = (
-            part_ref[block, :, kept].astype(jnp.float32) + theirs[block].astype(jnp.float32)
-        ).astype(jnp.bfloat16)
-
-        @pl.when(block != me)
-        def _():
-            home(block).start()
-
-        return carry
-
-    lax.fori_loop(1, count + 1, add, 0)
-    back_ref[me] = total[me]
-
-    def finish(block, carry):
-        pair(block).wait_send()
-
-        @pl.when(block != me)
-        def _():
-            home_arrival(block).wait_recv()
-            home(block).wait_send()
-
-        return carry
-
-    lax.fori_loop(0, count, finish, 0)
-
-
-def combine(part):
-    count, slots, width = part.shape
-    shape = (count, slots, width // 2)
-    return pl.pallas_call(
-        functools.partial(combine_kernel, count),
-        name="combine",
-        out_shape=jax.ShapeDtypeStruct(shape, jnp.bfloat16),
-        in_specs=[pl.BlockSpec(memory_space=pltpu.VMEM)],
-        out_specs=pl.BlockSpec(memory_space=pltpu.VMEM),
-        scratch_shapes=[pltpu.VMEM(shape, jnp.bfloat16)] * 2
-        + [pltpu.SemaphoreType.DMA((count,))] * 4,
-        compiler_params=pltpu.CompilerParams(
-            collective_id=3, has_side_effects=True, vmem_limit_bytes=grant(shape, shape, shape, part.shape, shape[1:])
-        ),
-    )(part)
+    )(packed, own, high, low, w_gate, w_up, w_down)
 
 
 def project_kernel(
@@ -526,21 +686,12 @@
     copies = jnp.broadcast_to(
         packed.reshape(EXPERTS, 1, CAP, half_width), (EXPERTS, chips, CAP, half_width)
     ).reshape(EXPERTS * chips, CAP, half_width)
-    rows_in = dispatch(copies).reshape(-1, D)
-    gate = jnp.dot(rows_in, w_gate, preferred_element_type=jnp.float32)
-    upward = jnp.dot(rows_in, w_up, preferred_element_type=jnp.float32)
-    inner = (jax.nn.silu(gate) * upward).astype(jnp.bfloat16)
-    inner = lax.optimization_barrier(inner)
-    part = jnp.dot(inner, w_down, preferred_element_type=jnp.float32).astype(jnp.bfloat16)
-    back = combine(part.reshape(seq_count, CAP, D)).reshape(EXPERTS, chips, CAP, half_width)
-    high = combine_weights.astype(jnp.bfloat16)
-    low = (combine_weights - high.astype(jnp.float32)).astype(jnp.bfloat16)
-    moe_out = jnp.zeros((tok_rows, half_width), jnp.float32)
-    for chip in range(chips):
-        piece = back[:, chip].reshape(EXPERTS * CAP, half_width)
-        moe_out = moe_out + jnp.dot(high, piece, preferred_element_type=jnp.float32)
-        moe_out = moe_out + jnp.dot(low, piece, preferred_element_type=jnp.float32)
-    return (own_rows + moe_out).astype(jnp.bfloat16)
+    spread = jnp.broadcast_to(
+        combine_weights.reshape(tok_rows, EXPERTS, 1, CAP), (tok_rows, EXPERTS, chips, CAP)
+    ).reshape(tok_rows, EXPERTS * chips * CAP)
+    high = spread.astype(jnp.bfloat16)
+    low = (spread - high.astype(jnp.float32)).astype(jnp.bfloat16)
+    return experts(copies, own_rows, high, low, w_gate, w_up, w_down)
 
 
 def solution(mesh):

time: 188 us -> 169 us (0.90); the launches traced: 184 us -> 168 us
  matrix products: 28.8 us -> 4.48 us
  Pallas kernels: 136 us -> 145 us
    dot_general x5 -> x0, matrix products: 25.4 us -> none  [the longest x1 9.59 us: per_device(): upward = jnp.dot(rows_in, w_up, preferred_element_type=jnp.float32)]
    pallas_call x2 -> x1, Pallas kernels: 51.4 us -> 59.9 us  [experts(): pl.pallas_call(functools.partial(experts_kernel, count), name='experts',...]
    reshape x2 -> x0, local copies, waits for them, and re-layouts: 3.04 us -> none  [the longest x1 1.62 us: per_device(): part.reshape(seq_count, CAP, D)]
  transfers between devices with their start and end apart: 1 -> 1, of which waited for: 1 -> 0; matrix products, arithmetic and copies ran while one was open for 1% -> 3% of each run, Pallas kernels for 0% -> 0%
where the time goes in v1:
time: 169 us; the launch traced here: 168 us
  Pallas kernels  145 us (86%)
  local copies, waits for them, and re-layouts  9.45 us (6%)
  starting transfers between devices  4.87 us (3%)
  other arithmetic  4.54 us (3%)
  matrix products  4.48 us (3%)
    pallas_call x1, Pallas kernels, experts(): pl.pallas_call(functools.partial(experts_kernel, count), name='experts',...  59.9 us
    pallas_call x1, Pallas kernels, project(): pl.pallas_call(functools.partial(project_kernel, count), name='project',...  59.5 us
    pallas_call x1, Pallas kernels, earlier_sums(): pl.pallas_call(functools.partial(sums_kernel, count), name='sums', out_sh...  25.1 us
    ppermute x1, starting transfers between devices, swap_heads(): return lax.ppermute(x, 'head', pairs)  4.87 us
    unnamed x24, local copies, waits for them, and re-layouts  3.65 us
  transfers between devices with their start and end apart: 1, of which 0 were waited for; matrix products, arithmetic and copies ran while one was open for 3% of the time, Pallas kernels for 0%

profile of v1, /device:TPU:27, one launch (start us, length us, event | category | flops | bytes accessed | tf_op | source)
XLA Modules:
  0.0 168.2 jit_solution(7800215773656596618)
XLA Ops:
  0.0 1.3 copy.67
  1.3 0.0 copy-start.3
  1.4 1.6 convolution_convert_fusion.1
  3.0 25.1 %sums.1 = bf16[8,256,128]{2,1,0:T(8,128)(2,1)S(1)} custom-call(bf16[8,256,128]{2,1,0:T(8,128)(2,1)S(1)} %bitcast.57), custom_call_target="tpu_custom_call" | custom-call | tf_op jit(solution)/shard_map/sums/pallas_call | solution.py:127
  28.1 0.5 convolution_bitcast_fusion.1
  28.6 0.0 copy-done.2
  28.6 0.0 copy-start.7
  28.6 1.9 %multiply_reduce_fusion.1 = (f32[128,16]{0,1:T(8,128)S(1)}, f32[128,16,128]{0,2,1:T(8,128)S(1)}) fusion(f32[128,16,128]{0,2,1:T(8,128)S(1)} %convolution_bitcast_fusion.1, bf16[128,16,128]{0,2,1:T(8,128)(2,1)S(1)} %bitcast.61, pred[128,128]{1,0:T(8,128)(4,1)S(1)} %iota_compare_fusion.1, bf16[128,2048]{1,0:T(8,128)(2,1)} %param.12, ...), kind=kOutput, calls=%fused_computation.11 | convolution fusion | flops 135526400 | bytes 3694592 | tf_op jit(solution)/shard_map/rbj,jrh->brh/dot_general | solution.py:646
  30.5 0.0 copy-start
  30.6 1.1 multiply_convert_fusion
  31.7 1.2 copy.66.shard_ref
  33.0 59.5 %project.1 = bf16[8,128,384]{2,1,0:T(8,128)(2,1)S(1)} custom-call(bf16[128,2048]{1,0:T(8,128)(2,1)S(1)} %copy.66.shard_ref, bf16[2048,384]{1,0:T(8,128)(2,1)S(1)} %copy-done), custom_call_target="tpu_custom_call" | custom-call | tf_op jit(solution)/shard_map/project/pallas_call | solution.py:587
  92.5 0.1 convert_bitcast_fusion
  92.6 0.0 copy-start.5
  92.6 0.2 copy.70
  92.8 0.8 copy-done.5
  93.6 0.1 add_dynamic-update-slice_fusion
  93.7 0.0 copy-start.9
  93.7 0.0 copy-start.10
  93.7 0.0 copy-start.8
  93.8 0.1 convert_element_type.75
  93.9 4.9 %collective-permute-start = (bf16[128,3072]{1,0:T(8,128)(2,1)S(1)}, bf16[128,3072]{1,0:T(8,128)(2,1)S(1)}, u32[]{:S(2)}, u32[]{:S(2)}) collective-permute-start(bf16[128,3072]{1,0:T(8,128)(2,1)S(1)} %convert_element_type.75), channel_id=1, source_target_pairs={{0,1},{1,0},{2,3},{3,2},{4,5},{5,4},{6,7},{7,6},{8,9},{9,8},{10,11... | collective-permute-start | bytes 2359304 | tf_op jit(solution)/shard_map/ppermute | solution.py:23
  98.7 0.0 copy-done.9
  98.7 0.1 copy.50
  98.8 0.1 eq.42
  99.0 0.1 eq.38
  99.1 0.6 reduce-window.6
  99.7 0.2 slice_reduce_fusion
  100.0 0.1 fusion.20
  100.1 0.1 reduce_sum.48
  100.2 0.1 copy.52
  100.3 0.7 select_reduce_fusion
  101.0 0.6 convert_element_type.82
  101.7 0.1 copy.63
  101.8 0.1 dynamic-slice.1
  101.9 1.0 copy.64.high_ref
  102.9 0.0 copy-start.4
  102.9 0.7 subtract_convert_fusion.low_ref
  103.5 0.0 collective-permute-done
  103.5 0.3 multiply_reduce_fusion
  103.9 0.0 copy-done.4
  103.9 0.0 copy-start.6
  103.9 0.1 constant_dynamic-slice_fusion.own_ref
  104.0 0.9 copy-done.1
  104.9 0.5 convolution_convert_fusion
  105.3 1.1 reshape_reshape.11.packed_ref
  106.5 59.9 %experts.1 = bf16[128,1536]{1,0:T(8,128)(2,1)} custom-call(bf16[8,36,1536]{2,1,0:T(8,128)(2,1)} %reshape_reshape.11.packed_ref, f32[128,1536]{1,0:T(8,128)} %copy-done.1, bf16[128,288]{1,0:T(8,128)(2,1)} %copy-done.4, bf16[128,288]{1,0:T(8,128)(2,1)} %subtract_convert_fusion.low_ref, bf16[3072,2304]{1,0:T(8,128)(2,1)} %gate_hbm.1, ...), custom_call_target="tpu_custom_call" | custom-call | tf_op jit(solution)/shard_map/experts/pallas_call | solution.py:416
  166.4 1.8 %copy.95 = bf16[128,1536]{1,0:T(8,128)(2,1)} copy(bf16[128,1536]{1,0:T(8,128)(2,1)} %experts.1) | data formatting | bytes 786432
  (15 shorter events, 0.1 us)
Async XLA Ops:
  1.3 26.8 %copy-start.3 = (bf16[128,2048]{1,0:T(8,128)(2,1)S(1)}, bf16[128,2048]{1,0:T(8,128)(2,1)}, u32[]{:S(2)}) copy-start(bf16[128,2048]{1,0:T(8,128)(2,1)} %param.12) | copy-start | bytes 1572868
  3.0 25.7 %copy-start.2 = (bf16[128,2048]{1,0:T(8,128)(2,1)S(1)}, bf16[128,2048]{1,0:T(8,128)(2,1)}, u32[]{:S(2)}) copy-start(bf16[128,2048]{1,0:T(8,128)(2,1)} %param.13) | copy-start | bytes 1572868
  28.6 1.9 %copy-start.7 = (f32[2048]{0:T(1024)S(1)}, f32[2048]{0:T(1024)}, u32[]{:S(2)}) copy-start(f32[2048]{0:T(1024)} %param.16) | copy-start | bytes 24580
  30.5 2.4 %copy-start = (bf16[2048,384]{1,0:T(8,128)(2,1)S(1)}, bf16[2048,384]{1,0:T(8,128)(2,1)}, u32[]{:S(2)}) copy-start(bf16[2048,384]{1,0:T(8,128)(2,1)} %weight_ref.1) | copy-start | bytes 4718596
  92.6 1.0 copy-start.5
  93.7 5.0 %copy-start.9 = (s32[128,2]{0,1:T(2,128)S(1)}, s32[128,2]{0,1:T(2,128)}, u32[]{:S(2)}) copy-start(s32[128,2]{0,1:T(2,128)} %param.19) | copy-start | bytes 3076
  93.7 6.6 %copy-start.10 = (f32[128,2]{0,1:T(2,128)S(1)}, f32[128,2]{0,1:T(2,128)}, u32[]{:S(2)}) copy-start(f32[128,2]{0,1:T(2,128)} %param.20) | copy-start | bytes 3076
  93.7 8.0 %copy-start.8 = (f32[3072]{0:T(1024)S(1)}, f32[3072]{0:T(1024)}, u32[]{:S(2)}) copy-start(f32[3072]{0:T(1024)} %param.18) | copy-start | bytes 36868
  93.9 9.7 %collective-permute-start = (bf16[128,3072]{1,0:T(8,128)(2,1)S(1)}, bf16[128,3072]{1,0:T(8,128)(2,1)S(1)}, u32[]{:S(2)}, u32[]{:S(2)}) collective-permute-start(bf16[128,3072]{1,0:T(8,128)(2,1)S(1)} %convert_element_type.75), channel_id=1, source_target_pairs={{0,1},{1,0},{2,3},{3,2},{4,5},{5,4},{6,7},{7,6},{8,9},{9,8},{10,11... | collective-permute-start | bytes 2359304 | tf_op jit(solution)/shard_map/ppermute | solution.py:23
  102.9 1.0 copy-start.4
  103.9 1.0 copy-start.6
  104.0 0.9 copy-start.1

commit v2 on v1

v2 whole, which is shorter than its diff:
```python
import functools

import jax
import jax.numpy as jnp
from jax import lax
from jax.experimental import pallas as pl
from jax.experimental.pallas import tpu as pltpu
from jax.sharding import PartitionSpec as P

D = 3072
HD = 128
EXPERTS = 8
TOP = 2
CAP = 36


EPS = 1e-06
VMEM_MOST = 61 << 20
TOGETHER = 2


def greet_all(me, count, pair=False):
    barrier = pltpu.get_barrier_semaphore()

    def greet(step, carry):
        pl.semaphore_signal(
            barrier,
            inc=1,
            device_id={"seq": lax.rem(me + step, count)},
            device_id_type=pl.DeviceIdType.MESH,
        )
        return carry

    lax.fori_loop(1, count, greet, 0)
    if pair:
        pl.semaphore_signal(
            barrier,
            inc=1,
            device_id={"head": 1 - lax.axis_index("head")},
            device_id_type=pl.DeviceIdType.MESH,
        )
    pl.semaphore_wait(barrier, count - 1 + int(pair))


def send_to(src, dst, send_sem, recv_sem, **device):
    return pltpu.make_async_remote_copy(
        src_ref=src,
        dst_ref=dst,
        send_sem=send_sem,
        recv_sem=recv_sem,
        device_id=device,
        device_id_type=pl.DeviceIdType.MESH,
    )


def tile_of(size, most):
    fits = [n for n in range(128, min(size, most) + 1, 128) if size % n == 0]
    return max(fits) if fits else size


def experts_kernel(
    count,
    packed_ref,
    own_ref,
    high_ref,
    low_ref,
    gate_hbm,
    up_hbm,
    down_hbm,
    mixed_ref,
    rows,
    x,
    gate,
    up,
    inner,
    w_gate,
    w_up,
    w_down,
    mine,
    theirs,
    part,
    total,
    back,
    send_sem,
    recv_sem,
    pair_send,
    pair_recv,
    part_send,
    part_recv,
    home_send,
    home_recv,
    gate_sem,
    up_sem,
    down_sem,
    own_sem,
):
    me, head = lax.axis_index("seq"), lax.axis_index("head")
    cap, half = packed_ref.shape[1], packed_ref.shape[2]
    chips = count // packed_ref.shape[0]
    chunks, wide = rows.shape[1], rows.shape[4]
    hidden = inner.shape[1]
    tile = tile_of(hidden, 768)
    group = 4
    span = group * cap

    def start_row(side, chunk):
        return pl.multiple_of(jnp.where(side == 0, head, 1 - head) * half + chunk * wide, wide)

    def weights(side, chunk):
        ks = pl.ds(start_row(side, chunk), wide)
        spot = chunk * 2 + side
        return (
            pltpu.make_async_copy(gate_hbm.at[ks], w_gate.at[ks], gate_sem.at[spot]),
            pltpu.make_async_copy(up_hbm.at[ks], w_up.at[ks], up_sem.at[spot]),
        )

    down = pltpu.make_async_copy(down_hbm, w_down, down_sem)

    def fetch(spot, carry):
        for copy in weights(lax.rem(spot, 2), spot // 2):
            copy.start()
        return carry

    lax.fori_loop(0, 2 * chunks, fetch, 0)
    down.start()
    greet_all(me, count, True)

    def chunk_of(chunk):
        return pl.ds(pl.multiple_of(chunk * wide, wide), wide)

    def out(chunk, other):
        return send_to(
            packed_ref.at[other // chips, :, chunk_of(chunk)],
            rows.at[0, chunk, me],
            send_sem.at[chunk, other],
            recv_sem.at[chunk, me],
            seq=other,
        )

    def arrival(chunk, other):
        return send_to(
            packed_ref.at[other // chips, :, chunk_of(chunk)],
            rows.at[0, chunk, other],
            send_sem.at[chunk, other],
            recv_sem.at[chunk, other],
            seq=other,
        )

    def keep(chunk):
        return pltpu.make_async_copy(
            packed_ref.at[me // chips, :, chunk_of(chunk)], rows.at[0, chunk, me], own_sem.at[chunk]
        )

    def pair(chunk):
        return send_to(
            rows.at[0, chunk], rows.at[1, chunk], pair_send.at[chunk], pair_recv.at[chunk], head=1 - head
        )

    def post(chunk, carry):
        def one(step, inside):
            out(chunk, lax.rem(me + step, count)).start()
            return inside

        lax.fori_loop(1, count, one, 0)
        keep(chunk).start()
        return carry

    lax.fori_loop(0, chunks, post, 0)
    gate[...] = jnp.zeros_like(gate)
    up[...] = jnp.zeros_like(up)

    def join(pages):
        return jnp.concatenate([page.astype(jnp.float32) for page in pages], axis=0).astype(jnp.bfloat16)

    def gather(side, chunk):
        def one(g, carry):
            x[pl.ds(pl.multiple_of(g * span, 16), span), :] = join(
                [rows[side, chunk, g * group + i] for i in range(group)]
            )
            return carry

        lax.fori_loop(0, count // group, one, 0)

    def accumulate(side, chunk):
        for copy in weights(side, chunk):
            copy.wait()
        gather(side, chunk)
        ks = pl.ds(start_row(side, chunk), wide)

        def one(n, carry):
            cols = pl.ds(pl.multiple_of(n * tile, tile), tile)
            gate[:, cols] += jnp.dot(x[...], w_gate[ks, cols], preferred_element_type=jnp.float32)
            up[:, cols] += jnp.dot(x[...], w_up[ks, cols], preferred_element_type=jnp.float32)
            return carry

        lax.fori_loop(0, hidden // tile, one, 0)

    def take(chunk, carry):
        def one(step, inside):
            arrival(chunk, lax.rem(me + count - step, count)).wait_recv()
            return inside

        lax.fori_loop(1, count, one, 0)
        keep(chunk).wait()
        pair(chunk).start()
        accumulate(0, chunk)
        pair(chunk).wait_recv()
        accumulate(1, chunk)
        return carry

    lax.fori_loop(0, chunks, take, 0)

    small = tile_of(hidden, 256)

    def activate(n, carry):
        cols = pl.ds(pl.multiple_of(n * small, small), small)
        inner[:, cols] = (jax.nn.silu(gate[:, cols]) * up[:, cols]).astype(jnp.bfloat16)
        return carry

    lax.fori_loop(0, hidden // small, activate, 0)
    down.wait()

    def hand(chunk):
        return send_to(mine.at[chunk], theirs.at[chunk], part_send.at[chunk], part_recv.at[chunk], head=1 - head)

    def home(chunk, other):
        return send_to(
            total.at[chunk, other],
            back.at[chunk, me],
            home_send.at[chunk, other],
            home_recv.at[chunk, me],
            seq=other,
        )

    def home_arrival(chunk, other):
        return send_to(
            total.at[chunk, other],
            back.at[chunk, other],
            home_send.at[chunk, other],
            home_recv.at[chunk, other],
            seq=other,
        )

    def project(side, chunk):
        cols = pl.ds(start_row(side, chunk), wide)
        part[...] = jnp.dot(inner[...], w_down[:, cols], preferred_element_type=jnp.float32)

    def give(chunk, carry):
        project(1, chunk)

        def split(g, inside):
            block = part[pl.ds(pl.multiple_of(g * span, 8), span), :]
            for i in range(group):
                mine[chunk, g * group + i] = block[i * cap : (i + 1) * cap].astype(jnp.bfloat16)
            return inside

        lax.fori_loop(0, count // group, split, 0)
        hand(chunk).start()
        project(0, chunk)
        hand(chunk).wait_recv()

        def add(g, inside):
            block = part[pl.ds(pl.multiple_of(g * span, 8), span), :]
            for i in range(group):
                spot = g * group + i
                total[chunk, spot] = (
                    block[i * cap : (i + 1) * cap] + theirs[chunk, spot].astype(jnp.float32)
                ).astype(jnp.bfloat16)
            return inside

        lax.fori_loop(0, count // group, add, 0)

        def one(step, inside):
            home(chunk, lax.rem(me + step, count)).start()
            return inside

        lax.fori_loop(1, count, one, 0)
        back[chunk, me] = total[chunk, me]
        return carry

    lax.fori_loop(0, chunks, give, 0)

    rows_of = (((0,), (0,)), ((), ()))

    def mix(chunk, carry):
        def one(step, inside):
            home_arrival(chunk, lax.rem(me + count - step, count)).wait_recv()
            return inside

        lax.fori_loop(1, count, one, 0)

        def pack(g, inside):
            x[pl.ds(pl.multiple_of(g * span, 16), span), :] = join(
                [back[chunk, g * group + i] for i in range(group)]
            )
            return inside

        lax.fori_loop(0, count // group, pack, 0)
        cols = chunk_of(chunk)
        mixed_ref[:, cols] = (
            own_ref[:, cols].astype(jnp.float32)
            + lax.dot_general(high_ref[...], x[...], rows_of, preferred_element_type=jnp.float32)
            + lax.dot_general(low_ref[...], x[...], rows_of, preferred_element_type=jnp.float32)
        ).astype(jnp.bfloat16)
        return carry

    lax.fori_loop(0, chunks, mix, 0)

    def finish(chunk, carry):
        def one(step, inside):
            other = lax.rem(me + step, count)
            out(chunk, other).wait_send()
            home(chunk, other).wait_send()
            return inside

        lax.fori_loop(1, count, one, 0)
        pair(chunk).wait_send()
        hand(chunk).wait_send()
        return carry

    lax.fori_loop(0, chunks, finish, 0)


def experts(packed, own, high, low, w_gate, w_up, w_down):
    count = lax.axis_size("seq")
    _, cap, half = packed.shape
    hidden = w_gate.shape[1]
    wide = tile_of(half, 512)
    chunks = half // wide
    rows = count * cap
    pages = (chunks, count, cap, wide)
    dma = pltpu.SemaphoreType.DMA
    vmem = pl.BlockSpec(memory_space=pltpu.VMEM)
    hbm = pl.BlockSpec(memory_space=pltpu.HBM)
    return pl.pallas_call(
        functools.partial(experts_kernel, count),
        name="experts",
        out_shape=jax.ShapeDtypeStruct(own.shape, jnp.bfloat16),
        in_specs=[vmem] * 4 + [hbm] * 3,
        out_specs=vmem,
        scratch_shapes=[
            pltpu.VMEM((2,) + pages, jnp.bfloat16),
            pltpu.VMEM((rows, wide), jnp.bfloat16),
            pltpu.VMEM((rows, hidden), jnp.float32),
            pltpu.VMEM((rows, hidden), jnp.float32),
            pltpu.VMEM((rows, hidden), jnp.bfloat16),
            pltpu.VMEM(w_gate.shape, jnp.bfloat16),
            pltpu.VMEM(w_up.shape, jnp.bfloat16),
            pltpu.VMEM(w_down.shape, jnp.bfloat16),
            pltpu.VMEM(pages, jnp.bfloat16),
            pltpu.VMEM(pages, jnp.bfloat16),
            pltpu.VMEM((rows, wide), jnp.float32),
            pltpu.VMEM(pages, jnp.bfloat16),
            pltpu.VMEM(pages, jnp.bfloat16),
            dma((chunks, count)),
            dma((chunks, count)),
            dma((chunks,)),
            dma((chunks,)),
            dma((chunks,)),
            dma((chunks,)),
            dma((chunks, count)),
            dma((chunks, count)),
            dma((2 * chunks,)),
            dma((2 * chunks,)),
            dma,
            dma((chunks,)),
        ],
        compiler_params=pltpu.CompilerParams(
            collective_id=2, has_side_effects=True, vmem_limit_bytes=VMEM_MOST
        ),
    )(packed, own, high, low, w_gate, w_up, w_down)


def mixer_kernel(
    count,
    query_hbm,
    keys_hbm,
    values_hbm,
    weight_hbm,
    resid_hbm,
    head_gain_ref,
    gain_ref,
    routes_ref,
    route_weights_ref,
    packed_ref,
    own_ref,
    high_ref,
    low_ref,
    query,
    keys,
    values,
    resid,
    weight,
    swap_give,
    swap_got,
    own_state,
    chain_got,
    chain_give,
    first_give,
    first_got,
    before,
    inside,
    normed,
    held,
    give,
    got,
    acc,
    cross_give,
    cross_got,
    home_give,
    home,
    square_give,
    square_got,
    load_sem,
    swap_send,
    swap_recv,
    chain_send,
    chain_recv,
    first_send,
    first_recv,
    w_send,
    w_recv,
    a_send,
    a_recv,
    pass_send,
    give_send,
    give_recv,
    cross_send,
    cross_recv,
    home_send,
    home_recv,
    square_send,
    square_recv,
):
    me, head = lax.axis_index("seq"), lax.axis_index("head")
    outer, inner = me // 2, lax.rem(me, 2)
    outers = count // 2
    partner = outer * 2 + (1 - inner)
    rows, width = query.shape
    quarter = width // 2
    heads = quarter // HD
    groups, together = swap_give.shape[0], swap_give.shape[1]
    same = head == inner
    cross = jnp.logical_not(same)
    kept = outers // 2
    target_head = outer // kept
    f32, bf16 = jnp.float32, jnp.bfloat16

    loads = [
        pltpu.make_async_copy(src, dst, load_sem.at[i])
        for i, (src, dst) in enumerate(
            ((keys_hbm, keys), (values_hbm, values), (query_hbm, query), (resid_hbm, resid))
        )
    ]
    for load in loads:
        load.start()

    barrier = pltpu.get_barrier_semaphore()

    def greet(**device):
        pl.semaphore_signal(barrier, inc=1, device_id=device, device_id_type=pl.DeviceIdType.MESH)

    def greet_column(step, carry):
        other = lax.rem(outer + step, outers) * 2 + inner
        greet(seq=other)
        greet(seq=other, head=1 - head)
        return carry

    lax.fori_loop(1, outers, greet_column, 0)
    greet(head=1 - head)
    greet(seq=partner)
    greet(seq=partner, head=1 - head)

    def lanes_of(n):
        return pl.ds(pl.multiple_of(n * HD, HD), HD)

    def state(n):
        return lax.dot_general(
            keys[:, lanes_of(n)],
            values[:, lanes_of(n)],
            (((0,), (0,)), ((), ())),
            preferred_element_type=f32,
        )

    loads[0].wait()
    loads[1].wait()

    def other_states(g, carry):
        for i in range(together):
            swap_give[g, i] = state((1 - inner) * heads + g * together + i).astype(bf16)
        return carry

    lax.fori_loop(0, groups, other_states, 0)
    pl.semaphore_wait(barrier, 2 * outers + 1)

    def swap(g):
        return send_to(swap_give.at[g], swap_got.at[g], swap_send.at[g], swap_recv.at[g], seq=partner)

    def chain(g):
        return send_to(chain_give.at[g], chain_got.at[g], chain_send.at[g], chain_recv.at[g], seq=me + 2)

    def first(g):
        return send_to(first_give.at[g], first_got.at[g], first_send.at[g], first_recv.at[g], seq=partner)

    def post(g, carry):
        swap(g).start()
        return carry

    lax.fori_loop(0, groups, post, 0)

    def cut(which):
        return pl.ds(pl.multiple_of(which * quarter, quarter), quarter)

    w_local = pltpu.make_async_copy(weight_hbm.at[cut(head)], weight.at[inner], w_recv.at[0])
    w_near = send_to(
        weight_hbm.at[cut(1 - head)], weight.at[inner], w_send.at[1], w_recv.at[0], head=1 - head
    )
    w_straight = send_to(
        weight_hbm.at[cut(head)], weight.at[inner], w_send.at[0], w_recv.at[1], seq=partner
    )
    w_turned = send_to(
        weight_hbm.at[cut(1 - head)],
        weight.at[inner],
        w_send.at[1],
        w_recv.at[1],
        seq=partner,
        head=1 - head,
    )

    @pl.when(same)
    def _():
        w_local.start()
        w_near.start()

    def own_states(g, carry):
        for i in range(together):
            own_state[g, i] = state(inner * heads + g * together + i)
        return carry

    lax.fori_loop(0, groups, own_states, 0)
    loads[2].wait()
    token = lax.broadcasted_iota(jnp.int32, (rows, rows), 0)
    causal = token >= lax.broadcasted_iota(jnp.int32, (rows, rows), 1)

    def within(n):
        scores = lax.dot_general(
            query[:, lanes_of(n)],
            keys[:, lanes_of(n)],
            (((1,), (1,)), ((), ())),
            preferred_element_type=f32,
        )
        masked = jnp.where(causal, scores, 0.0).astype(bf16)
        inside[n] = jnp.dot(masked, values[:, lanes_of(n)], preferred_element_type=f32)

    def link(g, carry):
        swap(g).wait_recv()

        @pl.when(outer > 0)
        def _():
            chain(g).wait_recv()

        start = jnp.where(outer > 0, chain_got[g].astype(f32), 0.0)
        mine, theirs = own_state[g], swap_got[g].astype(f32)
        chain_give[g] = (start + mine + theirs).astype(bf16)
        first_give[g] = (start + jnp.where(inner == 0, mine, 0.0)).astype(bf16)
        before[g] = (start + jnp.where(inner == 1, theirs, 0.0)).astype(bf16)

        @pl.when(outer + 1 < outers)
        def _():
            chain(g).start()

        first(g).start()
        for i in range(2 * together):
            within(g * 2 * together + i)
        return carry

    @pl.when(outer == 0)
    def _():
        chain_got[...] = jnp.zeros_like(chain_got)

    lax.fori_loop(0, groups, link, 0)

    def attend(n, prefix):
        attention = inside[n] + jnp.dot(query[:, lanes_of(n)], prefix, preferred_element_type=f32)
        scale = lax.rsqrt(jnp.mean(attention * attention, axis=-1, keepdims=True) + EPS)
        normed[:, lanes_of(n)] = (attention * scale * head_gain_ref[:, lanes_of(n)]).astype(bf16)

    def attend_first(g, carry):
        for i in range(together):
            attend(inner * heads + g * together + i, before[g, i])
        return carry

    lax.fori_loop(0, groups, attend_first, 0)

    def a_remote(which, recv, **device):
        return send_to(
            normed.at[:, cut(which)], held.at[outer, inner], a_send.at[0], a_recv.at[outer, inner], **device
        )

    a_local = pltpu.make_async_copy(
        normed.at[:, cut(inner)], held.at[outer, inner], a_recv.at[outer, inner]
    )
    a_turned = a_remote(inner, 1, seq=partner, head=1 - head)
    a_near = send_to(
        normed.at[:, cut(1 - inner)],
        held.at[outer, inner],
        a_send.at[1],
        a_recv.at[outer, inner],
        head=1 - head,
    )
    a_straight = send_to(
        normed.at[:, cut(1 - inner)],
        held.at[outer, inner],
        a_send.at[1],
        a_recv.at[outer, inner],
        seq=partner,
    )

    @pl.when(same)
    def _():
        a_local.start()

    @pl.when(cross)
    def _():
        a_turned.start()

    def attend_second(g, carry):
        first(g).wait_recv()
        for i in range(together):
            attend((1 - inner) * heads + g * together + i, first_got[g, i])
        return carry

    lax.fori_loop(0, groups, attend_second, 0)

    @pl.when(same)
    def _():
        a_near.start()

    @pl.when(cross)
    def _():
        a_straight.start()
        w_straight.start()
        w_turned.start()

    experts_count, cap = packed_ref.shape[0], packed_ref.shape[1]
    places = high_ref.shape[0]
    chips = count // experts_count
    expert = lax.broadcasted_iota(jnp.int32, (16, rows), 0)
    names = [routes_ref[j : j + 1, :] for j in range(TOP)]
    marks = sum((expert == name).astype(f32) for name in names)
    later = (token < lax.broadcasted_iota(jnp.int32, (rows, rows), 1)).astype(bf16)
    ahead = jnp.dot(marks.astype(bf16), later, preferred_element_type=f32)
    slots = [
        jnp.sum(jnp.where(expert == name, ahead, 0.0), axis=0, keepdims=True).astype(jnp.int32)
        for name in names
    ]
    place = lax.broadcasted_iota(jnp.int32, (places, rows), 0)
    factors = jnp.zeros((places, rows), f32)
    for j in range(TOP):
        for chip in range(chips):
            hit = place == (names[j] * chips + chip) * cap + slots[j]
            factors = factors + jnp.where(hit, route_weights_ref[j : j + 1, :], 0.0)
    high = factors.astype(bf16)
    high_ref[...] = high
    low_ref[...] = (factors - high.astype(f32)).astype(bf16)

    def move(source, side, up):
        return send_to(
            held.at[source, side],
            held.at[source, side],
            pass_send.at[source, side, up],
            a_recv.at[source, side],
            seq=me + (2 if up else -2),
        )

    def forward(source, side):
        @pl.when((source <= outer) & (outer + 1 < outers))
        def _():
            move(source, side, 1).start()

        @pl.when((source >= outer) & (outer > 0))
        def _():
            move(source, side, 0).start()

    def arrive(source):
        for turn in range(2):
            side = head if turn == 0 else 1 - head
            move(source, side, 0).wait_recv()
            forward(source, side)

    def own_near():
        @pl.when(same)
        def _():
            a_local.wait()

        @pl.when(cross)
        def _():
            a_near.wait_recv()

        forward(outer, inner)

    def own_far():
        send_to(
            normed.at[:, cut(0)], held.at[outer, 1 - inner], a_send.at[0], a_recv.at[outer, 1 - inner], seq=partner
        ).wait_recv()
        forward(outer, 1 - inner)

    @pl.when(same)
    def _():
        own_near()
        own_far()

    @pl.when(cross)
    def _():
        own_far()
        own_near()

    def hand(source):
        return send_to(give.at[source], got.at[source], give_send.at[source], give_recv.at[source], head=1 - head)

    def over(source):
        return send_to(
            cross_give.at[source], cross_got.at[source], cross_send.at[source], cross_recv.at[source], seq=partner
        )

    spot = lax.rem(outer, kept) * 2 + head

    def home_to(source):
        return send_to(
            home_give.at[source],
            home.at[spot],
            home_send.at[source],
            home_recv.at[spot],
            seq=source * 2 + inner,
            head=target_head,
        )

    home_own = pltpu.make_async_copy(home_give.at[outer], home.at[spot], home_recv.at[spot])
    stays = head == target_head

    def multiply(source):
        block = held[source].reshape(2 * rows, quarter)
        give[source] = (
            jnp.dot(block, weight[1 - head], preferred_element_type=f32)
            .astype(bf16)
            .reshape(give.shape[1:])
        )
        hand(source).start()
        acc[source] = jnp.dot(block, weight[head], preferred_element_type=f32).reshape(acc.shape[1:])

    def reduce_pair(source):
        hand(source).wait_recv()
        cross_give[source] = (
            acc[source, 1 - inner] + got[source, 1 - inner].astype(f32)
        ).astype(bf16)
        over(source).start()
        acc[source, inner] = acc[source, inner] + got[source, inner].astype(f32)

    def send_home(source):
        over(source).wait_recv()
        home_give[source] = (acc[source, inner] + cross_got[source].astype(f32)).astype(bf16)

        @pl.when((source == outer) & stays)
        def _():
            home_own.start()

        @pl.when(jnp.logical_not((source == outer) & stays))
        def _():
            home_to(source).start()

    def near(distance, action):
        @pl.when((outer - distance >= 0) & (distance > 0))
        def _():
            action(outer - distance)

        @pl.when(outer + distance < outers)
        def _():
            action(outer + distance)

    near(1, arrive)

    @pl.when(same)
    def _():
        w_local.wait()

    @pl.when(cross)
    def _():
        w_near.wait_recv()

    send_to(
        weight_hbm.at[cut(0)], weight.at[1 - inner], w_send.at[0], w_recv.at[1], seq=partner
    ).wait_recv()
    multiply(outer)
    near(1, multiply)
    reduce_pair(outer)
    near(1, reduce_pair)
    send_home(outer)

    def step(distance, carry):
        near(distance, arrive)
        near(distance, multiply)
        near(distance - 1, send_home)
        near(distance, reduce_pair)
        return carry

    lax.fori_loop(2, outers, step, 0)
    near(outers - 1, send_home)

    def collect(piece, carry):
        source = head * kept + piece // 2
        local = (source == outer) & (lax.rem(piece, 2) == head)

        @pl.when(local)
        def _():
            home_own.wait()

        @pl.when(jnp.logical_not(local))
        def _():
            send_to(
                home_give.at[0], home.at[piece], home_send.at[0], home_recv.at[piece], head=1 - head
            ).wait_recv()

        return carry

    lax.fori_loop(0, 2 * kept, collect, 0)
    loads[3].wait()
    projected = jnp.concatenate([home[piece].astype(f32) for piece in range(2 * kept)], axis=1)
    hidden = (projected + resid[...].astype(f32)).astype(bf16)
    own_ref[...] = hidden
    wide = hidden.astype(f32)
    square = jnp.sum(wide * wide, axis=1, keepdims=True)
    square_give[...] = jnp.broadcast_to(square, square_give.shape)
    trade = send_to(square_give, square_got, square_send, square_recv, head=1 - head)
    trade.start()
    pick = lax.broadcasted_iota(jnp.int32, (experts_count * cap, rows), 0)
    picker = sum((pick == names[j] * cap + slots[j]).astype(f32) for j in range(TOP)).astype(bf16)
    trade.wait_recv()
    half = resid.shape[1]
    scale = lax.rsqrt((square + square_got[:, 0:1]) / (2 * half) + EPS)
    gain = gain_ref[:, pl.ds(pl.multiple_of(head * half, half), half)]
    moe_in = (wide * scale * gain).astype(bf16)
    chosen = jnp.dot(picker, moe_in, preferred_element_type=f32)
    for page in range(experts_count):
        packed_ref[page] = chosen[page * cap : (page + 1) * cap].astype(bf16)

    trade.wait_send()

    @pl.when(same)
    def _():
        w_near.wait_send()
        a_near.wait_send()

    @pl.when(cross)
    def _():
        w_straight.wait_send()
        w_turned.wait_send()
        a_turned.wait_send()
        a_straight.wait_send()

    def finish_group(g, carry):
        swap(g).wait_send()
        first(g).wait_send()

        @pl.when(outer + 1 < outers)
        def _():
            chain(g).wait_send()

        return carry

    lax.fori_loop(0, groups, finish_group, 0)

    def finish(source, carry):
        hand(source).wait_send()
        over(source).wait_send()

        @pl.when(jnp.logical_not((source == outer) & stays))
        def _():
            home_to(source).wait_send()

        for side in range(2):

            @pl.when((source <= outer) & (outer + 1 < outers))
            def _():
                move(source, side, 1).wait_send()

            @pl.when((source >= outer) & (outer > 0))
            def _():
                move(source, side, 0).wait_send()

        return carry

    lax.fori_loop(0, outers, finish, 0)


def mixer(query, keys, values, out_weight, resid, attn_gain, moe_gain, routes, route_weights):
    count = lax.axis_size("seq")
    outers = count // 2
    rows, width = query.shape
    columns = out_weight.shape[1]
    half = resid.shape[1]
    heads = width // HD // 2
    together = TOGETHER
    groups = heads // together
    dma = pltpu.SemaphoreType.DMA
    vmem = pl.BlockSpec(memory_space=pltpu.VMEM)
    hbm = pl.BlockSpec(memory_space=pltpu.HBM)
    bf16, f32 = jnp.bfloat16, jnp.float32
    states = (groups, together, HD, HD)
    return pl.pallas_call(
        functools.partial(mixer_kernel, count),
        name="mixer",
        out_shape=(
            jax.ShapeDtypeStruct((EXPERTS, CAP, half), bf16),
            jax.ShapeDtypeStruct((rows, half), bf16),
            jax.ShapeDtypeStruct((count * CAP, rows), bf16),
            jax.ShapeDtypeStruct((count * CAP, rows), bf16),
        ),
        in_specs=[hbm] * 5 + [vmem] * 4,
        out_specs=(vmem,) * 4,
        scratch_shapes=[
            pltpu.VMEM((rows, width), bf16),
            pltpu.VMEM((rows, width), bf16),
            pltpu.VMEM((rows, width), bf16),
            pltpu.VMEM((rows, half), bf16),
            pltpu.VMEM((2, width // 2, columns), bf16),
            pltpu.VMEM(states, bf16),
            pltpu.VMEM(states, bf16),
            pltpu.VMEM(states, f32),
            pltpu.VMEM(states, bf16),
            pltpu.VMEM(states, bf16),
            pltpu.VMEM(states, bf16),
            pltpu.VMEM(states, bf16),
            pltpu.VMEM(states, bf16),
            pltpu.VMEM((2 * heads, rows, HD), f32),
            pltpu.VMEM((rows, width), bf16),
            pltpu.VMEM((outers, 2, rows, width // 2), bf16),
            pltpu.VMEM((outers, 2, rows, columns), bf16),
            pltpu.VMEM((outers, 2, rows, columns), bf16),
            pltpu.VMEM((outers, 2, rows, columns), f32),
            pltpu.VMEM((outers, rows, columns), bf16),
            pltpu.VMEM((outers, rows, columns), bf16),
            pltpu.VMEM((outers, rows, columns), bf16),
            pltpu.VMEM((outers, rows, columns), bf16),
            pltpu.VMEM((rows, 128), f32),
            pltpu.VMEM((rows, 128), f32),
            dma((4,)),
            dma((groups,)),
            dma((groups,)),
            dma((groups,)),
            dma((groups,)),
            dma((groups,)),
            dma((groups,)),
            dma((2,)),
            dma((2,)),
            dma((2,)),
            dma((outers, 2)),
            dma((outers, 2, 2)),
            dma((outers,)),
            dma((outers,)),
            dma((outers,)),
            dma((outers,)),
            dma((outers,)),
            dma((outers,)),
            dma,
            dma,
        ],
        compiler_params=pltpu.CompilerParams(
            collective_id=0, has_side_effects=True, vmem_limit_bytes=63 << 20
        ),
    )(
        query,
        keys,
        values,
        out_weight,
        resid,
        attn_gain.reshape(1, width),
        moe_gain.reshape(1, 2 * half),
        routes.T,
        route_weights.T,
    )


def per_device(
    query,
    keys,
    values,
    resid,
    attn_gain,
    out_weight,
    moe_gain,
    routes,
    route_weights,
    w_gate,
    w_up,
    w_down,
):
    packed, own, high, low = mixer(
        query, keys, values, out_weight, resid, attn_gain, moe_gain, routes, route_weights
    )
    return experts(packed, own, high, low, w_gate, w_up, w_down)


def solution(mesh):
    return jax.shard_map(
        per_device,
        mesh=mesh,
        in_specs=(
            P(("grp", "seq"), "head"),
            P(("grp", "seq"), "head"),
            P(("grp", "seq"), "head"),
            P(("grp", "seq"), "head"),
            P("head"),
            P("head", "seq"),
            P(),
            P(("grp", "seq"), None),
            P(("grp", "seq"), None),
            P(None, ("seq", "head")),
            P(None, ("seq", "head")),
            P(("seq", "head"), None),
        ),
        out_specs=P(("grp", "seq"), "head"),
        check_vma=False,
    )
```

time: 169 us -> 141 us (0.83)
  local copies, waits for them, and re-layouts: 9.45 us -> 1.77 us
  Pallas kernels: 145 us -> 139 us
  starting transfers between devices: 4.87 us -> 0 us
  other arithmetic: 4.54 us -> 0 us
  matrix products: 4.48 us -> 0 us
    pallas_call x2 -> x1, Pallas kernels: 84.6 us -> 77 us  [mixer(): pl.pallas_call(functools.partial(mixer_kernel, count), name='mixer', out_...]
    ppermute x1 -> x0, starting transfers between devices: 4.87 us -> none  [swap_heads(): return lax.ppermute(x, 'head', pairs)]
    dot_general x4 -> x0, matrix products: 4.48 us -> none  [the longest x1 1.91 us: per_device(): jnp.einsum('rbj,jrh->brh', resident_weight_parts, value_three_dims, prefe...]
    reshape x2 -> x0, local copies, waits for them, and re-layouts: 2.56 us -> none  [the longest x1 1.31 us: per_device(): value_three_dims = values.reshape(tok_rows, local_heads, HD)]
    convert_element_type x5 -> x0, other arithmetic: 2.52 us -> none  [the longest x1 1.13 us: per_device(): normed = (attention * scale * attn_gain.reshape(local_heads, HD)).astype(...]
    pallas_call x1, Pallas kernels: 59.9 us -> 62 us  [experts(): pl.pallas_call(functools.partial(experts_kernel, count), name='experts',...]
    unnamed x24 -> x1, local copies, waits for them, and re-layouts: 3.65 us -> 1.77 us
  transfers between devices with their start and end apart: 1 -> 0, of which waited for: 0 -> 0; matrix products, arithmetic and copies ran while one was open for 3% -> 0% of each run, Pallas kernels for 0% -> 0%
where the time goes in v2:
time: 141 us
  Pallas kernels  139 us (99%)
  local copies, waits for them, and re-layouts  1.77 us (1%)
    pallas_call x1, Pallas kernels, mixer(): pl.pallas_call(functools.partial(mixer_kernel, count), name='mixer', out_...  77 us
    pallas_call x1, Pallas kernels, experts(): pl.pallas_call(functools.partial(experts_kernel, count), name='experts',...  62 us

profile of v2, /device:TPU:27, one launch (start us, length us, event | category | flops | bytes accessed | tf_op | source)
XLA Modules:
  0.0 140.8 jit_solution(3898800393769087355)
XLA Ops:
  0.0 77.0 %mixer.1 = (bf16[8,36,1536]{2,1,0:T(8,128)(2,1)}, bf16[128,1536]{1,0:T(8,128)(2,1)}, bf16[288,128]{1,0:T(8,128)(2,1)}, bf16[288,128]{1,0:T(8,128)(2,1)}) custom-call(bf16[128,2048]{1,0:T(8,128)(2,1)} %query_hbm.1, bf16[128,2048]{1,0:T(8,128)(2,1)} %keys_hbm.1, bf16[128,2048]{1,0:T(8,128)(2,1)} %values_hbm.1, bf16[2048,384]{1,0:T(8,128)(2,1)} %weight_hbm.1, ...), custom_call_target="tpu_custom_call" | custom-call | tf_op jit(solution)/shard_map/mixer/pallas_call | solution.py:909
  77.1 62.0 %experts.1 = bf16[128,1536]{1,0:T(8,128)(2,1)} custom-call(bf16[8,36,1536]{2,1,0:T(8,128)(2,1)} %get-tuple-element.9.packed_ref, bf16[128,1536]{1,0:T(8,128)(2,1)} %get-tuple-element.10.own_ref, bf16[288,128]{1,0:T(8,128)(2,1)} %get-tuple-element.11.high_ref, bf16[288,128]{1,0:T(8,128)(2,1)} %get-tuple-element.12.low_ref, bf16[3072,2304]{1,0:T(8,128)(2,1)} %gate_hbm.1, ...), custom_call_target="tpu_custom_call" | custom-call | tf_op jit(solution)/shard_map/experts/pallas_call | solution.py:335
  139.0 1.8 %copy.14 = bf16[128,1536]{1,0:T(8,128)(2,1)} copy(bf16[128,1536]{1,0:T(8,128)(2,1)} %experts.1) | data formatting | bytes 786432

commit v3 on v2

v3 whole, which is shorter than its diff:
```python
import functools

import jax
import jax.numpy as jnp
from jax import lax
from jax.experimental import pallas as pl
from jax.experimental.pallas import tpu as pltpu
from jax.sharding import PartitionSpec as P

D = 3072
HD = 128
EXPERTS = 8
TOP = 2
CAP = 36


EPS = 1e-06
VMEM_MOST = 67043328
TOGETHER = 2


def send_to(src, dst, send_sem, recv_sem, **device):
    return pltpu.make_async_remote_copy(
        src_ref=src,
        dst_ref=dst,
        send_sem=send_sem,
        recv_sem=recv_sem,
        device_id=device,
        device_id_type=pl.DeviceIdType.MESH,
    )


def tile_of(size, most):
    fits = [n for n in range(128, min(size, most) + 1, 128) if size % n == 0]
    return max(fits) if fits else size


class Tiles:
    def __init__(self, ref, row, col, rows, cols, lead, down):
        self.ref, self.row, self.col, self.rows, self.cols, self.lead, self.down = (
            ref, row, col, rows, cols, lead, down
        )

    def view(self, *index):
        flat, span = 0, 1
        for size, place in zip(self.lead, index):
            flat = flat * size + place
        for size in self.lead[len(index) :]:
            flat, span = flat * size, span * size
        if self.down:
            tall = self.rows * span
            start = flat * self.rows if isinstance(flat, int) else pl.multiple_of(flat * self.rows, self.rows)
            return self.ref.at[pl.ds(self.row + start, tall), pl.ds(self.col, self.cols)]
        start = flat * self.cols if isinstance(flat, int) else pl.multiple_of(flat * self.cols, self.cols)
        return self.ref.at[pl.ds(self.row, self.rows), pl.ds(self.col + start, self.cols * span)]

    def __getitem__(self, index):
        return self.view(*(index if isinstance(index, tuple) else (index,)))[...]

    def __setitem__(self, index, value):
        self.view(*(index if isinstance(index, tuple) else (index,)))[...] = value

    def clear(self):
        whole = self.view()
        whole[...] = jnp.zeros(whole.shape, whole.dtype)

    @property
    def at(self):
        return Views(self)


class Views:
    def __init__(self, tiles):
        self.tiles = tiles

    def __getitem__(self, index):
        return self.tiles.view(*(index if isinstance(index, tuple) else (index,)))


def spot_of(spot, w_down, gate, up):
    return ((w_down, gate, up)[spot[0]],) + spot[1:]


def plan_of(rows, width, half, columns, count):
    outers, quarter = count // 2, width // 2
    heads = quarter // HD
    lead = (heads // TOGETHER, TOGETHER)
    side = columns % 128 == 0
    right, below = width, 4 * rows
    lower = below + outers * 2 * rows
    flat = (rows, width, (1,), True)
    state = (HD, HD, lead, True)
    pair = (rows, columns, (outers, 2), True)
    line = (rows, columns, (outers,), True)
    plan = [(flat, (0, i * rows, 0)) for i in range(4)]
    plan.append(((rows, half, (1,), True), (0, lower, 0)))
    plan.append(((quarter, columns, (2,), True), (0, 0, right)))
    plan += [(state, (0, below, quarter + i * HD)) for i in range(7)]
    plan.append(((rows, quarter, (outers, 2), True), (0, below, 0)))
    plan += [(pair, (0, i * outers * 2 * rows, right + columns)) for i in range(2)]
    plan += [(line, (0, lower + rows, i * columns)) for i in range(4)]
    plan.append(((rows, HD, (2 * heads,), False), (1, 0, 0)))
    plan.append(((HD, HD, lead, False), (2, 0, 0)))
    plan += [((rows, columns, (outers,), not side), (2 - i, rows, 0)) for i in range(2)]
    return plan


def extent(shape, spot):
    rows, cols, lead, down = shape
    size = 1
    for n in lead:
        size = size * n
    tall, long = (rows * size, cols) if down else (rows, cols * size)
    return tall, long, spot[1] + tall, spot[2] + long


def layer_kernel(
    count,
    plan,
    query_hbm,
    keys_hbm,
    values_hbm,
    weight_hbm,
    resid_hbm,
    head_gain_ref,
    gain_ref,
    routes_ref,
    route_weights_ref,
    gate_hbm,
    up_hbm,
    down_hbm,
    mixed_ref,
    packed_ref,
    high_ref,
    low_ref,
    square_give,
    square_got,
    pages,
    x,
    gate,
    up,
    active,
    w_gate,
    w_up,
    w_down,
    mine,
    theirs,
    part,
    back,
    send_sem,
    recv_sem,
    pair_send,
    pair_recv,
    part_send,
    part_recv,
    home_send,
    home_recv,
    gate_sem,
    up_sem,
    down_sem,
    own_sem,
    load_sem,
    swap_send,
    swap_recv,
    chain_send,
    chain_recv,
    first_send,
    first_recv,
    w_send,
    w_recv,
    a_send,
    a_recv,
    pass_send,
    give_send,
    give_recv,
    cross_send,
    cross_recv,
    mhome_send,
    mhome_recv,
    square_send,
    square_recv,
    *extras,
):
    me, head = lax.axis_index("seq"), lax.axis_index("head")
    cap, half = packed_ref.shape[1], packed_ref.shape[2]
    chips = count // packed_ref.shape[0]
    chunks, wide = pages.shape[1], pages.shape[4]
    hidden = active.shape[1]
    tile = tile_of(hidden, 2304)
    group = 4
    span = group * cap

    def start_row(side, chunk):
        return pl.multiple_of(jnp.where(side == 0, head, 1 - head) * half + chunk * wide, wide)

    def weights(side, chunk):
        ks = pl.ds(start_row(side, chunk), wide)
        spot = chunk * 2 + side
        return (
            pltpu.make_async_copy(gate_hbm.at[ks], w_gate.at[ks], gate_sem.at[spot]),
            pltpu.make_async_copy(up_hbm.at[ks], w_up.at[ks], up_sem.at[spot]),
        )

    down = pltpu.make_async_copy(down_hbm, w_down, down_sem)

    def fetch(spot, carry):
        for copy in weights(lax.rem(spot, 2), spot // 2):
            copy.start()
        return carry

    def prefetch():
        lax.fori_loop(0, 2 * chunks, fetch, 0)

    (
        query,
        keys,
        values,
        normed,
        resid,
        weight,
        swap_give,
        swap_got,
        chain_got,
        chain_give,
        first_give,
        first_got,
        before,
        held,
        give,
        got,
        cross_give,
        cross_got,
        home_give,
        home,
        inside,
        own_state,
        acc_mine,
        acc_other,
    ) = (
        Tiles(*(spot if extra is None else (extra, 0, 0)), *shape)
        for extra, (shape, spot) in zip(
            extras or [None] * len(plan), ((shape, spot_of(spot, w_down, gate, up)) for shape, spot in plan)
        )
    )
    query, keys, values, normed, resid = (tiles.view(0) for tiles in (query, keys, values, normed, resid))

    outer, inner = me // 2, lax.rem(me, 2)
    outers = count // 2
    partner = outer * 2 + (1 - inner)
    rows, width = query_hbm.shape
    quarter = width // 2
    heads = quarter // HD
    together = TOGETHER
    groups = heads // together
    same = head == inner
    cross = jnp.logical_not(same)
    kept = outers // 2
    target_head = outer // kept
    f32, bf16 = jnp.float32, jnp.bfloat16

    loads = [
        pltpu.make_async_copy(src, dst, load_sem.at[i])
        for i, (src, dst) in enumerate(
            ((keys_hbm, keys), (values_hbm, values), (query_hbm, query), (resid_hbm, resid))
        )
    ]
    for load in loads:
        load.start()

    barrier = pltpu.get_barrier_semaphore()

    def greet(**device):
        pl.semaphore_signal(barrier, inc=1, device_id=device, device_id_type=pl.DeviceIdType.MESH)

    def greet_column(step, carry):
        other = lax.rem(outer + step, outers) * 2 + inner
        greet(seq=other)
        greet(seq=other, head=1 - head)
        return carry

    def greet_rest(step, carry):
        other = lax.rem(outer + step, outers) * 2 + 1 - inner
        greet(seq=other)
        return carry

    lax.fori_loop(1, outers, greet_column, 0)
    lax.fori_loop(1, outers, greet_rest, 0)
    greet(head=1 - head)
    greet(seq=partner)
    greet(seq=partner, head=1 - head)

    def lanes_of(n):
        return pl.ds(pl.multiple_of(n * HD, HD), HD)

    def state(n):
        return lax.dot_general(
            keys[:, lanes_of(n)],
            values[:, lanes_of(n)],
            (((0,), (0,)), ((), ())),
            preferred_element_type=f32,
        )

    loads[0].wait()
    loads[1].wait()

    def other_states(g, carry):
        for i in range(together):
            swap_give[g, i] = state((1 - inner) * heads + g * together + i).astype(bf16)
        return carry

    lax.fori_loop(0, groups, other_states, 0)
    pl.semaphore_wait(barrier, 3 * outers)

    def swap(g):
        return send_to(swap_give.at[g], swap_got.at[g], swap_send.at[g], swap_recv.at[g], seq=partner)

    def chain(g):
        return send_to(chain_give.at[g], chain_got.at[g], chain_send.at[g], chain_recv.at[g], seq=me + 2)

    def first(g):
        return send_to(first_give.at[g], first_got.at[g], first_send.at[g], first_recv.at[g], seq=partner)

    def post(g, carry):
        swap(g).start()
        return carry

    lax.fori_loop(0, groups, post, 0)
    prefetch()

    def cut(which):
        return pl.ds(pl.multiple_of(which * quarter, quarter), quarter)

    w_local = pltpu.make_async_copy(weight_hbm.at[cut(head)], weight.at[inner], w_recv.at[0])
    w_near = send_to(
        weight_hbm.at[cut(1 - head)], weight.at[inner], w_send.at[1], w_recv.at[0], head=1 - head
    )
    w_straight = send_to(
        weight_hbm.at[cut(head)], weight.at[inner], w_send.at[0], w_recv.at[1], seq=partner
    )
    w_turned = send_to(
        weight_hbm.at[cut(1 - head)],
        weight.at[inner],
        w_send.at[1],
        w_recv.at[1],
        seq=partner,
        head=1 - head,
    )

    @pl.when(same)
    def _():
        w_local.start()
        w_near.start()

    def own_states(g, carry):
        for i in range(together):
            own_state[g, i] = state(inner * heads + g * together + i)
        return carry

    lax.fori_loop(0, groups, own_states, 0)
    loads[2].wait()
    token = lax.broadcasted_iota(jnp.int32, (rows, rows), 0)
    causal = token >= lax.broadcasted_iota(jnp.int32, (rows, rows), 1)

    def within(n):
        scores = lax.dot_general(
            query[:, lanes_of(n)],
            keys[:, lanes_of(n)],
            (((1,), (1,)), ((), ())),
            preferred_element_type=f32,
        )
        masked = jnp.where(causal, scores, 0.0).astype(bf16)
        inside[n] = jnp.dot(masked, values[:, lanes_of(n)], preferred_element_type=f32)

    def link(g, carry):
        swap(g).wait_recv()

        @pl.when(outer > 0)
        def _():
            chain(g).wait_recv()

        for i in range(together):
            start = jnp.where(outer > 0, chain_got[g, i].astype(f32), 0.0)
            mine, theirs = own_state[g, i], swap_got[g, i].astype(f32)
            chain_give[g, i] = (start + mine + theirs).astype(bf16)
            first_give[g, i] = (start + jnp.where(inner == 0, mine, 0.0)).astype(bf16)
            before[g, i] = (start + jnp.where(inner == 1, theirs, 0.0)).astype(bf16)

        @pl.when(outer + 1 < outers)
        def _():
            chain(g).start()

        first(g).start()
        for i in range(2 * together):
            within(g * 2 * together + i)
        return carry

    @pl.when(outer == 0)
    def _():
        chain_got.clear()

    lax.fori_loop(0, groups, link, 0)

    def attend(n, prefix):
        attention = inside[n] + jnp.dot(query[:, lanes_of(n)], prefix, preferred_element_type=f32)
        scale = lax.rsqrt(jnp.mean(attention * attention, axis=-1, keepdims=True) + EPS)
        normed[:, lanes_of(n)] = (attention * scale * head_gain_ref[:, lanes_of(n)]).astype(bf16)

    def attend_first(g, carry):
        for i in range(together):
            attend(inner * heads + g * together + i, before[g, i])
        return carry

    lax.fori_loop(0, groups, attend_first, 0)

    def a_remote(which, recv, **device):
        return send_to(
            normed.at[:, cut(which)], held.at[outer, inner], a_send.at[0], a_recv.at[outer, inner], **device
        )

    a_local = pltpu.make_async_copy(
        normed.at[:, cut(inner)], held.at[outer, inner], a_recv.at[outer, inner]
    )
    a_turned = a_remote(inner, 1, seq=partner, head=1 - head)
    a_near = send_to(
        normed.at[:, cut(1 - inner)],
        held.at[outer, inner],
        a_send.at[1],
        a_recv.at[outer, inner],
        head=1 - head,
    )
    a_straight = send_to(
        normed.at[:, cut(1 - inner)],
        held.at[outer, inner],
        a_send.at[1],
        a_recv.at[outer, inner],
        seq=partner,
    )

    @pl.when(same)
    def _():
        a_local.start()

    @pl.when(cross)
    def _():
        a_turned.start()

    def attend_second(g, carry):
        first(g).wait_recv()
        for i in range(together):
            attend((1 - inner) * heads + g * together + i, first_got[g, i])
        return carry

    lax.fori_loop(0, groups, attend_second, 0)

    @pl.when(same)
    def _():
        a_near.start()

    @pl.when(cross)
    def _():
        a_straight.start()
        w_straight.start()
        w_turned.start()

    experts_count = packed_ref.shape[0]
    places = high_ref.shape[0]
    expert = lax.broadcasted_iota(jnp.int32, (16, rows), 0)
    names = [routes_ref[j : j + 1, :] for j in range(TOP)]
    marks = sum((expert == name).astype(f32) for name in names)
    later = (token < lax.broadcasted_iota(jnp.int32, (rows, rows), 1)).astype(bf16)
    ahead = jnp.dot(marks.astype(bf16), later, preferred_element_type=f32)
    slots = [
        jnp.sum(jnp.where(expert == name, ahead, 0.0), axis=0, keepdims=True).astype(jnp.int32)
        for name in names
    ]
    place = lax.broadcasted_iota(jnp.int32, (places, rows), 0)
    factors = jnp.zeros((places, rows), f32)
    for j in range(TOP):
        for chip in range(chips):
            hit = place == (names[j] * chips + chip) * cap + slots[j]
            factors = factors + jnp.where(hit, route_weights_ref[j : j + 1, :], 0.0)
    high = factors.astype(bf16)
    high_ref[...] = high
    low_ref[...] = (factors - high.astype(f32)).astype(bf16)

    def move(source, side, up):
        return send_to(
            held.at[source, side],
            held.at[source, side],
            pass_send.at[source, side, up],
            a_recv.at[source, side],
            seq=me + (2 if up else -2),
        )

    def forward(source, side):
        @pl.when((source <= outer) & (outer + 1 < outers))
        def _():
            move(source, side, 1).start()

        @pl.when((source >= outer) & (outer > 0))
        def _():
            move(source, side, 0).start()

    def arrive(source):
        for turn in range(2):
            side = head if turn == 0 else 1 - head
            move(source, side, 0).wait_recv()
            forward(source, side)

    def own_near():
        @pl.when(same)
        def _():
            a_local.wait()

        @pl.when(cross)
        def _():
            a_near.wait_recv()

        forward(outer, inner)

    def own_far():
        send_to(
            normed.at[:, cut(0)], held.at[outer, 1 - inner], a_send.at[0], a_recv.at[outer, 1 - inner], seq=partner
        ).wait_recv()
        forward(outer, 1 - inner)

    @pl.when(same)
    def _():
        own_near()
        own_far()

    @pl.when(cross)
    def _():
        own_far()
        own_near()

    def hand(source):
        return send_to(give.at[source], got.at[source], give_send.at[source], give_recv.at[source], head=1 - head)

    def over(source):
        return send_to(
            cross_give.at[source], cross_got.at[source], cross_send.at[source], cross_recv.at[source], seq=partner
        )

    spot = lax.rem(outer, kept) * 2 + head

    def home_to(source):
        return send_to(
            home_give.at[source],
            home.at[spot],
            mhome_send.at[source],
            mhome_recv.at[spot],
            seq=source * 2 + inner,
            head=target_head,
        )

    home_own = pltpu.make_async_copy(home_give.at[outer], home.at[spot], mhome_recv.at[spot])
    stays = head == target_head

    def multiply(source):
        block = held[source]
        give[source] = jnp.dot(block, weight[1 - head], preferred_element_type=f32).astype(bf16)
        hand(source).start()
        both = jnp.dot(block, weight[head], preferred_element_type=f32)
        acc_mine[source] = jnp.where(inner == 0, both[:rows], both[rows:])
        acc_other[source] = jnp.where(inner == 0, both[rows:], both[:rows])

    def reduce_pair(source):
        hand(source).wait_recv()
        cross_give[source] = (
            acc_other[source] + got[source, 1 - inner].astype(f32)
        ).astype(bf16)
        over(source).start()
        acc_mine[source] = acc_mine[source] + got[source, inner].astype(f32)

    def send_home(source):
        over(source).wait_recv()
        home_give[source] = (acc_mine[source] + cross_got[source].astype(f32)).astype(bf16)

        @pl.when((source == outer) & stays)
        def _():
            home_own.start()

        @pl.when(jnp.logical_not((source == outer) & stays))
        def _():
            home_to(source).start()

    def near(distance, action):
        @pl.when((outer - distance >= 0) & (distance > 0))
        def _():
            action(outer - distance)

        @pl.when(outer + distance < outers)
        def _():
            action(outer + distance)

    near(1, arrive)

    @pl.when(same)
    def _():
        w_local.wait()

    @pl.when(cross)
    def _():
        w_near.wait_recv()

    send_to(
        weight_hbm.at[cut(0)], weight.at[1 - inner], w_send.at[0], w_recv.at[1], seq=partner
    ).wait_recv()
    multiply(outer)
    near(1, multiply)
    reduce_pair(outer)
    near(1, reduce_pair)
    send_home(outer)

    def step(distance, carry):
        near(distance, arrive)
        near(distance, multiply)
        near(distance - 1, send_home)
        near(distance, reduce_pair)
        return carry

    lax.fori_loop(2, outers, step, 0)
    near(outers - 1, send_home)

    def collect(piece, carry):
        source = head * kept + piece // 2
        local = (source == outer) & (lax.rem(piece, 2) == head)

        @pl.when(local)
        def _():
            home_own.wait()

        @pl.when(jnp.logical_not(local))
        def _():
            send_to(
                home_give.at[0], home.at[piece], mhome_send.at[0], mhome_recv.at[piece], head=1 - head
            ).wait_recv()

        return carry

    lax.fori_loop(0, 2 * kept, collect, 0)
    loads[3].wait()
    projected = jnp.concatenate([home[piece].astype(f32) for piece in range(2 * kept)], axis=1)
    stream = (projected + resid[...].astype(f32)).astype(bf16)
    mixed_ref[...] = stream
    broad = stream.astype(f32)
    square = jnp.sum(broad * broad, axis=1, keepdims=True)
    square_give[...] = jnp.broadcast_to(square, square_give.shape)
    trade = send_to(square_give, square_got, square_send, square_recv, head=1 - head)
    trade.start()
    pick = lax.broadcasted_iota(jnp.int32, (experts_count * cap, rows), 0)
    picker = sum((pick == names[j] * cap + slots[j]).astype(f32) for j in range(TOP)).astype(bf16)
    trade.wait_recv()
    scale = lax.rsqrt((square + square_got[:, 0:1]) / (2 * half) + EPS)
    gain = gain_ref[:, pl.ds(pl.multiple_of(head * half, half), half)]
    moe_in = (broad * scale * gain).astype(bf16)
    chosen = jnp.dot(picker, moe_in, preferred_element_type=f32)
    for page in range(experts_count):
        packed_ref[page] = chosen[page * cap : (page + 1) * cap].astype(bf16)

    trade.wait_send()

    @pl.when(same)
    def _():
        w_near.wait_send()
        a_near.wait_send()

    @pl.when(cross)
    def _():
        w_straight.wait_send()
        w_turned.wait_send()
        a_turned.wait_send()
        a_straight.wait_send()

    def finish_group(g, carry):
        swap(g).wait_send()
        first(g).wait_send()

        @pl.when(outer + 1 < outers)
        def _():
            chain(g).wait_send()

        return carry

    lax.fori_loop(0, groups, finish_group, 0)

    def finish(source, carry):
        hand(source).wait_send()
        over(source).wait_send()

        @pl.when(jnp.logical_not((source == outer) & stays))
        def _():
            home_to(source).wait_send()

        for side in range(2):

            @pl.when((source <= outer) & (outer + 1 < outers))
            def _():
                move(source, side, 1).wait_send()

            @pl.when((source >= outer) & (outer > 0))
            def _():
                move(source, side, 0).wait_send()

        return carry

    lax.fori_loop(0, outers, finish, 0)

    down.start()

    def chunk_of(chunk):
        return pl.ds(pl.multiple_of(chunk * wide, wide), wide)

    def out(chunk, other):
        return send_to(
            packed_ref.at[other // chips, :, chunk_of(chunk)],
            pages.at[0, chunk, me],
            send_sem.at[chunk, other],
            recv_sem.at[chunk, me],
            seq=other,
        )

    def arrival(chunk, other):
        return send_to(
            packed_ref.at[other // chips, :, chunk_of(chunk)],
            pages.at[0, chunk, other],
            send_sem.at[chunk, other],
            recv_sem.at[chunk, other],
            seq=other,
        )

    def keep(chunk):
        return pltpu.make_async_copy(
            packed_ref.at[me // chips, :, chunk_of(chunk)], pages.at[0, chunk, me], own_sem.at[chunk]
        )

    def pair_copy(chunk):
        return send_to(
            pages.at[0, chunk], pages.at[1, chunk], pair_send.at[chunk], pair_recv.at[chunk], head=1 - head
        )

    def post(chunk, carry):
        def one(step, inside):
            out(chunk, lax.rem(me + step, count)).start()
            return inside

        lax.fori_loop(1, count, one, 0)
        keep(chunk).start()
        return carry

    lax.fori_loop(0, chunks, post, 0)
    gate[...] = jnp.zeros_like(gate)
    up[...] = jnp.zeros_like(up)

    def join(pages):
        return jnp.concatenate([page.astype(jnp.float32) for page in pages], axis=0).astype(jnp.bfloat16)

    def gather(side, chunk):
        def one(g, carry):
            x[pl.ds(pl.multiple_of(g * span, 16), span), :] = join(
                [pages[side, chunk, g * group + i] for i in range(group)]
            )
            return carry

        lax.fori_loop(0, count // group, one, 0)

    def accumulate(side, chunk):
        for copy in weights(side, chunk):
            copy.wait()
        gather(side, chunk)
        ks = pl.ds(start_row(side, chunk), wide)

        def one(n, carry):
            cols = pl.ds(pl.multiple_of(n * tile, tile), tile)
            gate[:, cols] += jnp.dot(x[...], w_gate[ks, cols], preferred_element_type=jnp.float32)
            up[:, cols] += jnp.dot(x[...], w_up[ks, cols], preferred_element_type=jnp.float32)
            return carry

        lax.fori_loop(0, hidden // tile, one, 0)

    def take(chunk, carry):
        def one(step, inside):
            arrival(chunk, lax.rem(me + count - step, count)).wait_recv()
            return inside

        lax.fori_loop(1, count, one, 0)
        keep(chunk).wait()
        pair_copy(chunk).start()
        accumulate(0, chunk)
        pair_copy(chunk).wait_recv()
        accumulate(1, chunk)
        return carry

    lax.fori_loop(0, chunks, take, 0)

    small = tile_of(hidden, 256)

    def activate(n, carry):
        cols = pl.ds(pl.multiple_of(n * small, small), small)
        active[:, cols] = (jax.nn.silu(gate[:, cols]) * up[:, cols]).astype(jnp.bfloat16)
        return carry

    lax.fori_loop(0, hidden // small, activate, 0)
    down.wait()

    def hand_part(chunk):
        return send_to(mine.at[chunk], theirs.at[chunk], part_send.at[chunk], part_recv.at[chunk], head=1 - head)

    def back_home(chunk, other):
        return send_to(
            mine.at[chunk, other],
            back.at[chunk, me],
            home_send.at[chunk, other],
            home_recv.at[chunk, me],
            seq=other,
        )

    def home_arrival(chunk, other):
        return send_to(
            mine.at[chunk, other],
            back.at[chunk, other],
            home_send.at[chunk, other],
            home_recv.at[chunk, other],
            seq=other,
        )

    def project(side, chunk):
        cols = pl.ds(start_row(side, chunk), wide)
        part[...] = jnp.dot(active[...], w_down[:, cols], preferred_element_type=jnp.float32)

    def give(chunk, carry):
        project(1, chunk)

        def split(g, inside):
            block = part[pl.ds(pl.multiple_of(g * span, 8), span), :]
            for i in range(group):
                mine[chunk, g * group + i] = block[i * cap : (i + 1) * cap].astype(jnp.bfloat16)
            return inside

        lax.fori_loop(0, count // group, split, 0)
        hand_part(chunk).start()
        project(0, chunk)
        hand_part(chunk).wait_recv()
        hand_part(chunk).wait_send()

        def add(g, inside):
            block = part[pl.ds(pl.multiple_of(g * span, 8), span), :]
            for i in range(group):
                spot = g * group + i
                mine[chunk, spot] = (
                    block[i * cap : (i + 1) * cap] + theirs[chunk, spot].astype(jnp.float32)
                ).astype(jnp.bfloat16)
            return inside

        lax.fori_loop(0, count // group, add, 0)

        def one(step, inside):
            back_home(chunk, lax.rem(me + step, count)).start()
            return inside

        lax.fori_loop(1, count, one, 0)
        back[chunk, me] = mine[chunk, me]
        return carry

    lax.fori_loop(0, chunks, give, 0)

    rows_of = (((0,), (0,)), ((), ()))

    def mix(chunk, carry):
        def one(step, inside):
            home_arrival(chunk, lax.rem(me + count - step, count)).wait_recv()
            return inside

        lax.fori_loop(1, count, one, 0)

        def pack(g, inside):
            x[pl.ds(pl.multiple_of(g * span, 16), span), :] = join(
                [back[chunk, g * group + i] for i in range(group)]
            )
            return inside

        lax.fori_loop(0, count // group, pack, 0)
        cols = chunk_of(chunk)
        mixed_ref[:, cols] = (
            mixed_ref[:, cols].astype(jnp.float32)
            + lax.dot_general(high_ref[...], x[...], rows_of, preferred_element_type=jnp.float32)
            + lax.dot_general(low_ref[...], x[...], rows_of, preferred_element_type=jnp.float32)
        ).astype(jnp.bfloat16)
        return carry

    lax.fori_loop(0, chunks, mix, 0)

    def finish_all(chunk, carry):
        def one(step, inside):
            other = lax.rem(me + step, count)
            out(chunk, other).wait_send()
            back_home(chunk, other).wait_send()
            return inside

        lax.fori_loop(1, count, one, 0)
        pair_copy(chunk).wait_send()
        return carry

    lax.fori_loop(0, chunks, finish_all, 0)


def layer(query, keys, values, out_weight, resid, attn_gain, moe_gain, routes, route_weights, w_gate, w_up, w_down):
    count = lax.axis_size("seq")
    outers = count // 2
    rows, width = query.shape
    columns = out_weight.shape[1]
    half = resid.shape[1]
    groups = width // HD // 2 // TOGETHER
    hidden = w_gate.shape[1]
    wide = tile_of(half, 512)
    chunks = half // wide
    slots = count * CAP
    pages = (chunks, count, CAP, wide)
    dma = pltpu.SemaphoreType.DMA
    vmem = pl.BlockSpec(memory_space=pltpu.VMEM)
    hbm = pl.BlockSpec(memory_space=pltpu.HBM)
    bf16, f32 = jnp.bfloat16, jnp.float32
    plan = plan_of(rows, width, half, columns, count)
    room = (w_down.shape, (slots, hidden), (slots, hidden))
    shared = columns % 128 == 0 and all(
        extent(shape, spot)[2] <= room[spot[0]][0] and extent(shape, spot)[3] <= room[spot[0]][1]
        for shape, spot in plan
    )
    extras = [
        pltpu.VMEM(extent(shape, spot)[:2], f32 if spot[0] else bf16) for shape, spot in plan if not shared
    ]
    return pl.pallas_call(
        functools.partial(layer_kernel, count, plan),
        name="layer",
        out_shape=jax.ShapeDtypeStruct((rows, half), bf16),
        in_specs=[hbm] * 5 + [vmem] * 4 + [hbm] * 3,
        out_specs=vmem,
        scratch_shapes=[
            pltpu.VMEM((EXPERTS, CAP, half), bf16),
            pltpu.VMEM((slots, rows), bf16),
            pltpu.VMEM((slots, rows), bf16),
            pltpu.VMEM((rows, 128), f32),
            pltpu.VMEM((rows, 128), f32),
            pltpu.VMEM((2,) + pages, bf16),
            pltpu.VMEM((slots, wide), bf16),
            pltpu.VMEM((slots, hidden), f32),
            pltpu.VMEM((slots, hidden), f32),
            pltpu.VMEM((slots, hidden), bf16),
            pltpu.VMEM(w_gate.shape, bf16),
            pltpu.VMEM(w_up.shape, bf16),
            pltpu.VMEM(w_down.shape, bf16),
            pltpu.VMEM(pages, bf16),
            pltpu.VMEM(pages, bf16),
            pltpu.VMEM((slots, wide), f32),
            pltpu.VMEM(pages, bf16),
            dma((chunks, count)),
            dma((chunks, count)),
            dma((chunks,)),
            dma((chunks,)),
            dma((chunks,)),
            dma((chunks,)),
            dma((chunks, count)),
            dma((chunks, count)),
            dma((2 * chunks,)),
            dma((2 * chunks,)),
            dma,
            dma((chunks,)),
            dma((4,)),
            dma((groups,)),
            dma((groups,)),
            dma((groups,)),
            dma((groups,)),
            dma((groups,)),
            dma((groups,)),
            dma((2,)),
            dma((2,)),
            dma((2,)),
            dma((outers, 2)),
            dma((outers, 2, 2)),
            dma((outers,)),
            dma((outers,)),
            dma((outers,)),
            dma((outers,)),
            dma((outers,)),
            dma((outers,)),
            dma,
            dma,
        ]
        + extras,
        compiler_params=pltpu.CompilerParams(
            collective_id=0, has_side_effects=True, vmem_limit_bytes=VMEM_MOST
        ),
    )(
        query,
        keys,
        values,
        out_weight,
        resid,
        attn_gain.reshape(1, width),
        moe_gain.reshape(1, 2 * half),
        routes.T,
        route_weights.T,
        w_gate,
        w_up,
        w_down,
    )


def per_device(
    query,
    keys,
    values,
    resid,
    attn_gain,
    out_weight,
    moe_gain,
    routes,
    route_weights,
    w_gate,
    w_up,
    w_down,
):
    return layer(
        query,
        keys,
        values,
        out_weight,
        resid,
        attn_gain,
        moe_gain,
        routes,
        route_weights,
        w_gate,
        w_up,
        w_down,
    )


def solution(mesh):
    return jax.shard_map(
        per_device,
        mesh=mesh,
        in_specs=(
            P(("grp", "seq"), "head"),
            P(("grp", "seq"), "head"),
            P(("grp", "seq"), "head"),
            P(("grp", "seq"), "head"),
            P("head"),
            P("head", "seq"),
            P(),
            P(("grp", "seq"), None),
            P(("grp", "seq"), None),
            P(None, ("seq", "head")),
            P(None, ("seq", "head")),
            P(("seq", "head"), None),
        ),
        out_specs=P(("grp", "seq"), "head"),
        check_vma=False,
    )
```

time: 141 us -> 133 us (0.943); the launches traced: 141 us -> 131 us
  Pallas kernels: 139 us -> 130 us
    pallas_call x2 -> x1, Pallas kernels: 139 us -> 130 us  [layer(): pl.pallas_call(functools.partial(layer_kernel, count, plan), name='layer'...]
where the time goes in v3:
time: 133 us; the launch traced here: 131 us
  Pallas kernels  130 us (98%)
  local copies, waits for them, and re-layouts  1.77 us (1%)
    pallas_call x1, Pallas kernels, layer(): pl.pallas_call(functools.partial(layer_kernel, count, plan), name='layer'...  130 us

profile of v3, /device:TPU:27, one launch (start us, length us, event | category | flops | bytes accessed | tf_op | source)
XLA Modules:
  0.0 131.3 jit_solution(1861378944679282867)
XLA Ops:
  0.0 129.6 %layer.1 = bf16[128,1536]{1,0:T(8,128)(2,1)} custom-call(bf16[128,2048]{1,0:T(8,128)(2,1)} %query_hbm.1, bf16[128,2048]{1,0:T(8,128)(2,1)} %keys_hbm.1, bf16[128,2048]{1,0:T(8,128)(2,1)} %values_hbm.1, bf16[2048,384]{1,0:T(8,128)(2,1)} %weight_hbm.1, bf16[128,1536]{1,0:T(8,128)(2,1)} %resid_hbm.1, f32[1,2048]{1,0:T(1,128)} %bitcast.5, f32[1,3072]{1,0:T(1,128)} %bitcast.4, ...), custom_call_target="tpu_custom_call" | custom-call | tf_op jit(solution)/shard_map/layer/pallas_call | solution.py:933
  129.6 1.8 %copy.14 = bf16[128,1536]{1,0:T(8,128)(2,1)} copy(bf16[128,1536]{1,0:T(8,128)(2,1)} %layer.1) | data formatting | bytes 786432
